TPU v7x, 512 devices: a whole 4x4x16 slice. The times are simulated.
512 devices in a mesh: shot: 16 (over x, y), tx: 4 (over z_hi, core), ty: 8 (over z_lo).
Axes of the slice: x: 4, y: 4, z: 16 (z_hi: 2, z_lo: 8; z = z_hi * 8 + z_lo), core: 2. Of those that a mesh axis runs over, the one named last changes fastest.
Arguments:
- forward_prev: float32 [16, 128, 64, 256], P('shot', 'tx', 'ty'), may hold values from -6 to 6
- forward_now: float32 [16, 128, 64, 256], P('shot', 'tx', 'ty'), may hold values from -6 to 6
- adjoint_prev: float32 [16, 128, 64, 256], P('shot', 'tx', 'ty'), may hold values from -6 to 6
- adjoint_now: float32 [16, 128, 64, 256], P('shot', 'tx', 'ty'), may hold values from -6 to 6
- velocity_model: bfloat16 [32, 512, 8, 256], P(('tx', 'ty'), 'shot'), may hold values from 1.5 to 4.5
- aperture: int32 [16, 32, 32], P('shot', ('tx', 'ty')), may hold values from 0 to 511, as said below
- source_cell: int32 [16, 2], P('shot'), may hold values from 0 to 127, as said below
- source_strength: float32 [16], P('shot'), may hold values from -60 to 60
- receiver_cell: int32 [16, 128, 2], P('shot'), may hold values from 0 to 127, as said below
- receiver_trace: float32 [16, 128], P('shot'), may hold values from -60 to 60
Outputs:
- forward_next: float32 [16, 128, 64, 256], P('shot', 'tx', 'ty')
- adjoint_next: float32 [16, 128, 64, 256], P('shot', 'tx', 'ty')
- image_slab: float32 [32, 512, 8, 256], P(('tx', 'ty'), 'shot')
Inputs may be any that keep to these rules, and one draw needn't show every extreme that they name: `aperture`: each list of 32 block ids (one shot, one tile position) names every owner, id // 32, at most 2 times, and some owner exactly 2 times. `source_cell`: first entry below 128, second below 64. `receiver_cell`: first entry below 128, second below 64; receivers may share a cell.
All inputs are finite; a program needn't handle non-finite values.
Results may differ from a plain program's by a relative error of at most 0.0004.
Values may be sent and summed in bfloat16 or wider, within the bound.
A program may use at most 64 MiB of HBM per device.

v0:
```python
import jax
import jax.numpy as jnp
from jax import lax
from jax.sharding import PartitionSpec as P

SURFACE_DEPTH = 8


STENCIL_WEIGHTS = (-205.0 / 72.0, 8.0 / 5.0, -1.0 / 5.0, 8.0 / 315.0, -1.0 / 560.0)
STEP_RATIO = 0.1


def padded_2(cells, sides, width):
    for axis, dim in sides:
        count = lax.axis_size(axis)
        ends = count - 1
        head = lax.slice_in_dim(cells, 0, width, axis=dim)
        tail = lax.slice_in_dim(cells, cells.shape[dim] - width, cells.shape[dim], axis=dim)
        cells = jnp.concatenate(
            [
                lax.ppermute(tail, axis, [(i, (i + 1) % count) for i in range(ends)]),
                cells,
                lax.ppermute(head, axis, [((i + 1) % count, i) for i in range(ends)]),
            ],
            axis=dim,
        )
    return cells


def laplacian(padded):
    extent_x = padded.shape[-3] - 8
    extent_y = padded.shape[-2] - 8
    extent_z = padded.shape[-1] - 8
    centre = padded[..., 4 : 4 + extent_x, 4 : 4 + extent_y, 4 : 4 + extent_z]
    summed = 3.0 * STENCIL_WEIGHTS[0] * centre
    for offset in range(1, 5):
        neighbours = (
            padded[..., 4 + offset : 4 + offset + extent_x, 4 : 4 + extent_y, 4 : 4 + extent_z]
            + padded[..., 4 - offset : 4 - offset + extent_x, 4 : 4 + extent_y, 4 : 4 + extent_z]
            + padded[..., 4 : 4 + extent_x, 4 + offset : 4 + offset + extent_y, 4 : 4 + extent_z]
            + padded[..., 4 : 4 + extent_x, 4 - offset : 4 - offset + extent_y, 4 : 4 + extent_z]
            + padded[..., 4 : 4 + extent_x, 4 : 4 + extent_y, 4 + offset : 4 + offset + extent_z]
            + padded[..., 4 : 4 + extent_x, 4 : 4 + extent_y, 4 - offset : 4 - offset + extent_z]
        )
        summed = summed + STENCIL_WEIGHTS[offset] * neighbours
    return summed


def injections(
    anchor_x, anchor_y, cells_x, cells_y, cells_z, source_xy, strength, receiver_xy, traces
):
    grid_x = lax.iota(jnp.int32, cells_x) + anchor_x
    grid_y = lax.iota(jnp.int32, cells_y) + anchor_y
    depth_mark = (lax.iota(jnp.int32, cells_z) == SURFACE_DEPTH).astype(jnp.float32)
    mark_x = (grid_x == source_xy[0]).astype(jnp.float32)
    mark_y = (grid_y == source_xy[1]).astype(jnp.float32)
    injected = strength * mark_x[:, None, None] * mark_y[None, :, None] * depth_mark[None, None, :]
    receiver_x = (receiver_xy[:, 0][:, None] == grid_x[None, :]).astype(jnp.float32) * traces[
        :, None
    ]
    receiver_y = (receiver_xy[:, 1][:, None] == grid_y[None, :]).astype(jnp.float32)
    surface = jnp.dot(receiver_x.T, receiver_y, precision=lax.Precision.HIGHEST)
    recorded = surface[:, :, None] * depth_mark[None, None, :]
    return (injected, recorded)


def on_device(
    forward_prev,
    forward_now,
    adjoint_prev,
    adjoint_now,
    velocity_model,
    aperture,
    source_cell,
    source_strength,
    receiver_cell,
    receiver_trace,
):
    shot_count = lax.axis_size("shot")
    cells_x = forward_now.shape[1]
    cells_y = forward_now.shape[2]
    cells_z = forward_now.shape[3]
    slab_rows = velocity_model.shape[1]
    capacity = max(2, cells_x // shot_count)
    slot_total = shot_count * capacity
    block_ids = aperture[0, 0]
    owners = block_ids // slab_rows
    local_ids = block_ids % slab_rows
    positions = lax.iota(jnp.int32, cells_x)
    earlier = (owners[:, None] == owners[None, :]) & (positions[None, :] < positions[:, None])
    ranking = jnp.sum(earlier.astype(jnp.int32), axis=1)
    slot_index = owners * capacity + ranking
    placed = slot_index[:, None] == lax.iota(jnp.int32, slot_total)[None, :]
    wanted = jnp.sum(jnp.where(placed, (local_ids + 1)[:, None], 0), axis=0) - 1
    incoming = lax.all_to_all(
        wanted.reshape(shot_count, capacity), "shot", split_axis=0, concat_axis=0, tiled=True
    )
    chosen = incoming.reshape(slot_total)[:, None] == lax.iota(jnp.int32, slab_rows)[None, :]
    blocks = jnp.dot(
        chosen.astype(jnp.bfloat16),
        velocity_model[0].reshape(slab_rows, cells_y * cells_z),
        preferred_element_type=jnp.float32,
    ).astype(jnp.bfloat16)
    arrived = lax.all_to_all(
        blocks.reshape(shot_count, capacity, cells_y * cells_z),
        "shot",
        split_axis=0,
        concat_axis=0,
        tiled=True,
    )
    velocity_tile = jnp.dot(
        placed.astype(jnp.bfloat16),
        arrived.reshape(slot_total, cells_y * cells_z),
        preferred_element_type=jnp.float32,
    )
    scaled = velocity_tile.reshape(cells_x, cells_y, cells_z) * STEP_RATIO
    courant = scaled * scaled
    stacked = jnp.concatenate([forward_now, adjoint_now], axis=0)
    padded = padded_2(stacked, (("tx", 1), ("ty", 2)), 4)
    padded = jnp.pad(padded, ((0, 0), (0, 0), (0, 0), (4, 4)))
    curvature = laplacian(padded)
    anchor_x = lax.axis_index("tx") * cells_x
    anchor_y = lax.axis_index("ty") * cells_y
    injected, recorded = injections(
        anchor_x,
        anchor_y,
        cells_x,
        cells_y,
        cells_z,
        source_cell[0],
        source_strength[0],
        receiver_cell[0],
        receiver_trace[0],
    )
    forward_next = 2.0 * forward_now[0] - forward_prev[0] + courant * (curvature[0] + injected)
    adjoint_next = 2.0 * adjoint_now[0] - adjoint_prev[0] + courant * (curvature[1] + recorded)
    correlation = (forward_next * adjoint_next).reshape(cells_x, cells_y * cells_z)
    row_ids = lax.iota(jnp.int32, slab_rows * lax.axis_size("shot"))
    matches = (row_ids[:, None] == block_ids[None, :]).astype(jnp.float32)
    image_part = lax.psum_scatter(
        jnp.dot(matches, correlation, precision=lax.Precision.HIGHEST),
        "shot",
        scatter_dimension=0,
        tiled=True,
    )
    image_slab = image_part.reshape(1, slab_rows, cells_y, cells_z)
    return (forward_next[None], adjoint_next[None], image_slab)


def solution(mesh):
    in_specs = (
        P("shot", "tx", "ty", None),
        P("shot", "tx", "ty", None),
        P("shot", "tx", "ty", None),
        P("shot", "tx", "ty", None),
        P(("tx", "ty"), "shot", None, None),
        P("shot", ("tx", "ty"), None),
        P("shot", None),
        P("shot"),
        P("shot", None, None),
        P("shot", None),
    )
    out_specs = (
        P("shot", "tx", "ty", None),
        P("shot", "tx", "ty", None),
        P(("tx", "ty"), "shot", None, None),
    )
    return jax.shard_map(
        on_device, mesh=mesh, in_specs=in_specs, out_specs=out_specs, check_vma=False
    )
```

profile of v0, /device:TPU:1, one launch (start us, length us, event | category | flops | bytes accessed | tf_op | source)
XLA Modules:
  0.0 165.8 jit_solution(16067681528286630654)
XLA Ops:
  7.2 1.0 copy_dynamic-update-slice_fusion.1
  8.2 1.0 copy_dynamic-update-slice_fusion
  9.3 8.8 %collective-permute-start = (f32[2,4,8,256]{3,1,2,0:T(4,128)S(1)}, f32[2,4,8,256]{3,1,2,0:T(4,128)S(1)}, u32[]{:S(2)}, u32[]{:S(2)}) collective-permute-start(f32[2,4,8,256]{3,1,2,0:T(4,128)S(1)} %get-tuple-element.22), channel_id=1, source_target_pairs={{8,0},{16,8},{24,16},{9,1},{17,9},{25,17},{10,2},{18,10},{26,18},{... | collective-permute-start | bytes 196616 | tf_op jit(solution)/shard_map/ppermute | solution.py:23
  18.1 10.0 %collective-permute-start.1 = (f32[2,4,8,256]{3,1,2,0:T(4,128)S(1)}, f32[2,4,8,256]{3,1,2,0:T(4,128)S(1)}, u32[]{:S(2)}, u32[]{:S(2)}) collective-permute-start(f32[2,4,8,256]{3,1,2,0:T(4,128)S(1)} %get-tuple-element.23), channel_id=1, source_target_pairs={{0,8},{8,16},{16,24},{1,9},{9,17},{17,25},{2,10},{10,18},{18,26},{... | collective-permute-start | bytes 196616 | tf_op jit(solution)/shard_map/ppermute | solution.py:21
  28.0 0.7 and_select_fusion.1
  28.7 0.2 convert_reduce_fusion
  28.9 0.1 select_reduce_fusion
  29.0 0.7 sub.27
  29.7 6.8 %all-to-all-start = ((s32[16,1,2]{2,1,0:T(1,128)}), s32[16,1,2]{2,1,0:T(1,128)S(1)}, u32[]{:S(2)}, u32[]{:S(2)}) async-start(s32[16,1,2]{2,1,0:T(1,128)} %bitcast.3), calls=%async_computation | async-start | bytes 16384 | tf_op jit(solution)/shard_map/all_to_all | solution.py:95
  36.5 1.3 fusion.63
  38.4 0.7 compare_convert_fusion.1
  39.1 0.8 slice_bitcast_fusion.3
  39.9 0.6 compare_select_fusion
  40.5 0.9 fusion.42
  41.5 0.9 copy.55
  42.4 0.4 all-to-all-done
  42.8 0.5 broadcast.241
  43.3 0.7 reduce.3
  44.0 0.1 eq.119
  44.1 0.2 convolution_convert_fusion
  44.3 0.8 reshape.200
  45.1 6.3 %all-to-all-start.1 = ((bf16[16,2,2048]{2,1,0:T(2,128)(2,1)}), bf16[16,2,2048]{2,1,0:T(2,128)(2,1)S(1)}, u32[]{:S(2)}, u32[]{:S(2)}) async-start(bf16[16,2,2048]{2,1,0:T(2,128)(2,1)} %reshape.200), calls=%async_computation.1 | async-start | bytes 262144 | tf_op jit(solution)/shard_map/all_to_all | solution.py:104
  51.4 0.0 reduce-scatter.2.cloned.1.call-start
  51.4 0.0 collective-permute-done.1
  51.4 0.1 pad_maximum_fusion.1
  51.6 1.3 collective-permute-start.2
  52.9 4.0 %collective-permute-start.3 = (f32[2,40,4,256]{3,1,2,0:T(8,128)S(1)}, f32[2,40,4,256]{3,1,2,0:T(8,128)S(1)}, u32[]{:S(2)}, u32[]{:S(2)}) collective-permute-start(f32[2,40,4,256]{3,1,2,0:T(8,128)S(1)} %get-tuple-element.20), channel_id=1, source_target_pairs={{0,1},{1,2},{2,3},{3,4},{4,5},{5,6},{6,7},{8,9},{9,10},{10,11},{11... | collective-permute-start | bytes 983048 | tf_op jit(solution)/shard_map/ppermute | solution.py:21
  56.9 0.1 broadcast_multiply_fusion
  56.9 1.1 all-to-all-done.1
  58.0 0.1 reshape.201
  58.1 1.3 collective-permute-done.2
  59.4 1.5 collective-permute-done.3
  60.9 0.2 pad_maximum_fusion
  61.0 0.7 select_maximum_fusion
  61.7 0.0 copy-start
  61.7 0.0 copy-start.1
  61.8 0.0 copy-start.2
  61.8 0.0 copy-start.3
  61.8 1.6 fusion.10
  63.4 0.0 copy-start.4
  63.4 0.5 multiply_bitcast_fusion
  64.0 0.1 copy-done.4
  64.0 3.7 %fusion.38 = f32[512,2048]{1,0:T(8,128)} fusion(f32[32,2048]{1,0:T(8,128)S(1)} %bitcast.69, s32[32]{0:T(128)S(1)} %bitcast.76), kind=kOutput, calls=%fused_computation.73 | convolution fusion | flops 402669568 | bytes 4456576 | tf_op jit(solution)/shard_map/dot_general | solution.py:141
  67.8 0.0 reduce-scatter.2.cloned.1.call-update
  67.8 0.9 copy.51
  68.6 0.9 copy.52
  69.5 87.7 %reduce-scatter.2.cloned.1.call-done = f32[32,2048]{1,0:T(8,128)} async-done(((f32[512,2048]{1,0:T(8,128)}), f32[32,2048]{1,0:T(8,128)}) %reduce-scatter.2.cloned.1.call-update) | async-done | bytes 262160 | tf_op jit(solution)/shard_map/reduce_scatter | solution.py:140
  157.2 1.7 %copy.56 = f32[4,8,8,256]{3,2,1,0:T(8,128)} copy(f32[4,8,8,256]{3,1,2,0:T(8,128)} %bitcast.72) | data formatting | bytes 524288
  (13 shorter events, 0.1 us)
Async XLA Ops:
  9.3 42.1 %collective-permute-start = (f32[2,4,8,256]{3,1,2,0:T(4,128)S(1)}, f32[2,4,8,256]{3,1,2,0:T(4,128)S(1)}, u32[]{:S(2)}, u32[]{:S(2)}) collective-permute-start(f32[2,4,8,256]{3,1,2,0:T(4,128)S(1)} %get-tuple-element.22), channel_id=1, source_target_pairs={{8,0},{16,8},{24,16},{9,1},{17,9},{25,17},{10,2},{18,10},{26,18},{... | collective-permute-start | bytes 196616 | tf_op jit(solution)/shard_map/ppermute | solution.py:23
  18.1 33.3 %collective-permute-start.1 = (f32[2,4,8,256]{3,1,2,0:T(4,128)S(1)}, f32[2,4,8,256]{3,1,2,0:T(4,128)S(1)}, u32[]{:S(2)}, u32[]{:S(2)}) collective-permute-start(f32[2,4,8,256]{3,1,2,0:T(4,128)S(1)} %get-tuple-element.23), channel_id=1, source_target_pairs={{0,8},{8,16},{16,24},{1,9},{9,17},{17,25},{2,10},{10,18},{18,26},{... | collective-permute-start | bytes 196616 | tf_op jit(solution)/shard_map/ppermute | solution.py:21
  29.7 13.1 %all-to-all-start = ((s32[16,1,2]{2,1,0:T(1,128)}), s32[16,1,2]{2,1,0:T(1,128)S(1)}, u32[]{:S(2)}, u32[]{:S(2)}) async-start(s32[16,1,2]{2,1,0:T(1,128)} %bitcast.3), calls=%async_computation | async-start | bytes 16384 | tf_op jit(solution)/shard_map/all_to_all | solution.py:95
  45.1 13.0 %all-to-all-start.1 = ((bf16[16,2,2048]{2,1,0:T(2,128)(2,1)}), bf16[16,2,2048]{2,1,0:T(2,128)(2,1)S(1)}, u32[]{:S(2)}, u32[]{:S(2)}) async-start(bf16[16,2,2048]{2,1,0:T(2,128)(2,1)} %reshape.200), calls=%async_computation.1 | async-start | bytes 262144 | tf_op jit(solution)/shard_map/all_to_all | solution.py:104
  51.4 105.8 %reduce-scatter.2.cloned.1.call-start = ((), (), s32[]{:S(2)}) async-start(), calls=%async_computation.3 | async-start | bytes 4456448 | tf_op jit(solution)/shard_map/reduce_scatter | solution.py:140
  51.6 7.8 %collective-permute-start.2 = (f32[2,40,4,256]{3,1,2,0:T(8,128)S(1)}, f32[2,40,4,256]{3,1,2,0:T(8,128)S(1)}, u32[]{:S(2)}, u32[]{:S(2)}) collective-permute-start(f32[2,40,4,256]{3,1,2,0:T(8,128)S(1)} %get-tuple-element.21), channel_id=1, source_target_pairs={{1,0},{2,1},{3,2},{4,3},{5,4},{6,5},{7,6},{9,8},{10,9},{11,10},{12... | collective-permute-start | bytes 983048 | tf_op jit(solution)/shard_map/ppermute | solution.py:23
  52.9 8.0 %collective-permute-start.3 = (f32[2,40,4,256]{3,1,2,0:T(8,128)S(1)}, f32[2,40,4,256]{3,1,2,0:T(8,128)S(1)}, u32[]{:S(2)}, u32[]{:S(2)}) collective-permute-start(f32[2,40,4,256]{3,1,2,0:T(8,128)S(1)} %get-tuple-element.20), channel_id=1, source_target_pairs={{0,1},{1,2},{2,3},{3,4},{4,5},{5,6},{6,7},{8,9},{9,10},{10,11},{11... | collective-permute-start | bytes 983048 | tf_op jit(solution)/shard_map/ppermute | solution.py:21
  61.7 1.6 copy-start
  61.7 1.6 copy-start.1
  61.8 1.6 copy-start.2
  61.8 1.6 copy-start.3
  63.4 0.7 copy-start.4
Sparse Core Ops, SparseCore 0:
  67.9 89.2 reduce-scatter.1
where the time goes:
time: 167 us; the launch traced here: 166 us
  waiting for transfers between devices  91.9 us (55%)
  starting transfers between devices  37.1 us (22%)
  between operations  15 us (9%)
  local copies, waits for them, and re-layouts  10.8 us (6%)
  other arithmetic  5.52 us (3%)
  matrix products  5.42 us (3%)
    reduce_scatter x1, waiting for transfers between devices, on_device(): lax.psum_scatter(jnp.dot(matches, correlation, precision=lax.Precision.HI...  87.7 us
    ppermute x2, starting transfers between devices, padded_2(): lax.ppermute(tail, axis, [(i, (i + 1) % count) for i in range(ends)])  14 us
    ppermute x2, starting transfers between devices, padded_2(): lax.ppermute(head, axis, [((i + 1) % count, i) for i in range(ends)])  10.1 us
    all_to_all x1, starting transfers between devices, on_device(): lax.all_to_all(wanted.reshape(shot_count, capacity), 'shot', split_axis=0...  6.75 us
    all_to_all x1, starting transfers between devices, on_device(): lax.all_to_all(blocks.reshape(shot_count, capacity, cells_y * cells_z), '...  6.28 us
    unnamed x15, local copies, waits for them, and re-layouts  5.52 us
    dot_general x1, matrix products, on_device(): jnp.dot(matches, correlation, precision=lax.Precision.HIGHEST)  3.74 us
  transfers between devices with their start and end apart: 7, of which 5 were waited for; matrix products, arithmetic and copies ran while one was open for 7% of the time, Pallas kernels for 0%

commit v1 on v0

v1 whole, which is shorter than its diff:
```python
import functools

import jax
import jax.numpy as jnp
import ml_dtypes
import numpy as np
from jax import lax
from jax.experimental import pallas as pl
from jax.experimental.pallas import tpu as pltpu
from jax.sharding import PartitionSpec as P

SURFACE_DEPTH = 8
STENCIL_WEIGHTS = (-205.0 / 72.0, 8.0 / 5.0, -1.0 / 5.0, 8.0 / 315.0, -1.0 / 560.0)
STEP_RATIO = 0.1
MESH = pl.DeviceIdType.MESH
NS, NTX, NTY = 16, 4, 8
CX, CY, CZ = 32, 8, 256
ROWS = CX * CY
SLAB = 32
NREC = 128
YH = CX * 4
XH = 4 * CY
HALO = 2 * YH + 2 * XH


def stencil_constants():
    w = np.array(STENCIL_WEIGHTS)
    band = np.zeros(600)
    band[1:5] = w[1:]
    row = np.arange(ROWS)
    x, y = row // CY, row % CY
    dx, dy = np.abs(x[:, None] - x[None, :]), np.abs(y[:, None] - y[None, :])
    inner = band[dx] * (dy == 0) + band[dy] * (dx == 0) + 3.0 * w[0] * ((dx == 0) & (dy == 0))
    z = np.arange(CZ)
    depth = band[np.abs(z[:, None] - z[None, :])]
    pick = np.zeros((ROWS, ROWS))
    halo = np.zeros((ROWS, 384))
    for cx in range(CX):
        for q in range(4):
            pick[cx * 4 + q, cx * CY + CY - 4 + q] = 1.0
            pick[YH + cx * 4 + q, cx * CY + q] = 1.0
            for cy in range(CY):
                halo[cx * CY + cy, cx * 4 + q] = band[cy + 4 - q]
                halo[cx * CY + cy, YH + cx * 4 + q] = band[CY + q - cy]
    for q in range(4):
        for cx in range(CX):
            for cy in range(CY):
                halo[cx * CY + cy, 2 * YH + q * CY + cy] = band[cx + 4 - q]
                halo[cx * CY + cy, 2 * YH + XH + q * CY + cy] = band[CX + q - cx]

    def parts(matrix):
        high = matrix.astype(np.float32).astype(ml_dtypes.bfloat16)
        low = (matrix - high.astype(np.float64)).astype(np.float32).astype(ml_dtypes.bfloat16)
        return [high, low]

    square = np.concatenate(parts(inner) + parts(depth) + parts(pick)[:1], axis=0)
    return square, np.concatenate(parts(halo), axis=0)


def mm(a, b):
    return jnp.dot(a, b, preferred_element_type=jnp.float32)


def kernel(
    f_prev, f_now, a_prev, a_now, velocity, aperture, source_cell, strength, receivers, traces,
    square_hbm, halo_hbm,
    f_out, a_out, image_out,
    now, prev, lap, high, low, slab_b, slab, ids, cell_v, trace_v, square, halo_w,
    pick_send, halo, tables, wanted, wanted_v, wanted_by, blocks, arrived, speed, corr_send, corr_in,
    hit, image,
    smem_tables, source_s, strength_s,
    load_sem, table_sem, id_send, id_recv, halo_send, halo_recv, v_send, v_recv, c_send, c_recv,
    out_sem,
):
    me = lax.axis_index("shot")
    tx = lax.axis_index("tx")
    ty = lax.axis_index("ty")

    loads = [
        pltpu.make_async_copy(aperture.at[0], ids, load_sem.at[0]),
        pltpu.make_async_copy(f_now.at[0], now.at[0], load_sem.at[1]),
        pltpu.make_async_copy(a_now.at[0], now.at[1], load_sem.at[2]),
        pltpu.make_async_copy(square_hbm, square, load_sem.at[3]),
        pltpu.make_async_copy(velocity.at[0], slab_b, load_sem.at[4]),
        pltpu.make_async_copy(halo_hbm, halo_w, load_sem.at[5]),
        pltpu.make_async_copy(f_prev.at[0], prev.at[0], load_sem.at[6]),
        pltpu.make_async_copy(a_prev.at[0], prev.at[1], load_sem.at[7]),
        pltpu.make_async_copy(receivers.at[0], cell_v, load_sem.at[8]),
        pltpu.make_async_copy(traces, trace_v, load_sem.at[9]),
        pltpu.make_async_copy(source_cell, source_s, load_sem.at[10]),
        pltpu.make_async_copy(strength, strength_s, load_sem.at[11]),
    ]
    for load in loads:
        load.start()

    barrier = pltpu.get_barrier_semaphore()

    @pl.loop(1, NS)
    def _(d):
        pl.semaphore_signal(
            barrier, inc=1, device_id={"shot": lax.rem(me + d, NS)}, device_id_type=MESH
        )

    sides = [
        (ty < NTY - 1, "ty", ty + 1),
        (ty > 0, "ty", ty - 1),
        (tx < NTX - 1, "tx", tx + 1),
        (tx > 0, "tx", tx - 1),
    ]
    for present, axis, other in sides:

        @pl.when(present)
        def _():
            pl.semaphore_signal(barrier, inc=1, device_id={axis: other}, device_id_type=MESH)

    for present, start, size in (
        (ty > 0, 0, YH),
        (ty < NTY - 1, YH, YH),
        (tx > 0, 2 * YH, XH),
        (tx < NTX - 1, 2 * YH + XH, XH),
    ):

        @pl.when(jnp.logical_not(present))
        def _():
            halo[:, start : start + size, :] = jnp.zeros((2, size, CZ), jnp.bfloat16)

    loads[0].wait()
    row_l = lax.broadcasted_iota(jnp.int32, (CX, CX), 1)
    row_s = lax.broadcasted_iota(jnp.int32, (CX, CX), 0)
    ids_l = jnp.broadcast_to(ids[...], (CX, CX))
    ids_s = ids_l.T
    earlier = ((ids_s >> 5) == (ids_l >> 5)) & (row_s < row_l)
    rank = jnp.sum(earlier.astype(jnp.int32), axis=0, keepdims=True)
    slot = 2 * (ids[...] >> 5) + rank
    placed = jnp.broadcast_to(slot, (CX, CX)).T == row_l
    tables[0, :, 0:CX] = slot
    tables[1, :, 0:CX] = jnp.sum(jnp.where(placed, row_s, 0), axis=0, keepdims=True)
    wanted[:, 0:CX] = jnp.sum(jnp.where(placed, ids_s & (SLAB - 1), 0), axis=0, keepdims=True)
    table_copy = pltpu.make_async_copy(tables, smem_tables, table_sem.at[0])
    table_copy.start()
    own_copy = pltpu.make_async_copy(wanted, wanted_by.at[me], table_sem.at[1])
    own_copy.start()

    for field in range(2):
        loads[1 + field].wait()
        u = now[field].reshape(ROWS, CZ)
        top = u.astype(jnp.bfloat16)
        high[field] = top
        low[field] = (u - top.astype(jnp.float32)).astype(jnp.bfloat16)
    loads[3].wait()
    for field in range(2):
        picked = mm(square[4 * ROWS : 5 * ROWS, :], high[field]).astype(jnp.bfloat16)
        pick_send[0, field] = picked[0:YH]
        pick_send[1, field] = picked[YH:]

    partners = (
        NS - 1
        + (ty > 0).astype(jnp.int32)
        + (ty < NTY - 1).astype(jnp.int32)
        + (tx > 0).astype(jnp.int32)
        + (tx < NTX - 1).astype(jnp.int32)
    )
    pl.semaphore_wait(barrier, partners)

    def id_copy(d):
        return pltpu.make_async_remote_copy(
            src_ref=wanted,
            dst_ref=wanted_v.at[me],
            send_sem=id_send.at[d],
            recv_sem=id_recv.at[d],
            device_id={"shot": lax.rem(me + d, NS)},
            device_id_type=MESH,
        )

    @pl.loop(1, NS)
    def _(d):
        id_copy(d).start()

    def halo_copy(n):
        axis, other = sides[n][1], sides[n][2]
        start = (0, YH, 2 * YH, 2 * YH + XH)[n]
        if n < 2:
            source, size = pick_send.at[n], YH
        else:
            source, size = high.at[:, pl.ds((CX - 4) * CY if n == 2 else 0, XH)], XH
        return pltpu.make_async_remote_copy(
            src_ref=source,
            dst_ref=halo.at[:, pl.ds(start, size)],
            send_sem=halo_send.at[n],
            recv_sem=halo_recv.at[n],
            device_id={axis: other},
            device_id_type=MESH,
        )

    for n in (2, 3, 0, 1):

        @pl.when(sides[n][0])
        def _():
            halo_copy(n).start()

    loads[4].wait()
    slab[...] = slab_b[...].astype(jnp.float32)

    own_copy.wait()
    depth_l = lax.broadcasted_iota(jnp.int32, (CY, ROWS), 1)
    same_y = (depth_l & (CY - 1)) == lax.broadcasted_iota(jnp.int32, (CY, ROWS), 0)
    block_l = jnp.where(same_y, depth_l >> 3, -1)

    def serve(shot):
        first = wanted_by[shot, 0, 2 * me]
        second = wanted_by[shot, 0, 2 * me + 1]
        pair = jnp.concatenate([slab[first], slab[second]], axis=0).astype(jnp.bfloat16)
        hits = jnp.concatenate([block_l == first, block_l == second], axis=0)
        hit[pl.ds(pl.multiple_of(shot * 16, 16), 16), :] = jnp.where(hits, 1.0, 0.0)
        return pair

    arrived[me] = serve(me)

    def block_copy(d):
        shot = lax.rem(me - d + NS, NS)
        return pltpu.make_async_remote_copy(
            src_ref=blocks.at[shot],
            dst_ref=arrived.at[me],
            send_sem=v_send.at[d],
            recv_sem=v_recv.at[d],
            device_id={"shot": shot},
            device_id_type=MESH,
        )

    @pl.loop(1, NS)
    def _(d):
        id_copy(d).wait_recv()
        shot = lax.rem(me - d + NS, NS)
        local = pltpu.make_async_copy(wanted_v.at[shot], wanted_by.at[shot], table_sem.at[1])
        local.start()
        local.wait()
        blocks[shot] = serve(shot)
        block_copy(d).start()

    for field in range(2):
        top, rest = high[field], low[field]
        lap[field] = (
            mm(square[0:ROWS, :], top)
            + mm(square[0:ROWS, :], rest)
            + mm(square[ROWS : 2 * ROWS, :], top)
            + mm(top, square[2 * ROWS : 3 * ROWS, :])
            + mm(rest, square[2 * ROWS : 3 * ROWS, :])
            + mm(top, square[3 * ROWS : 4 * ROWS, :])
        ).reshape(CX, CY, CZ)

    for load in loads[8:]:
        load.wait()
    row = lax.broadcasted_iota(jnp.int32, (ROWS, 1), 0)

    def local_row(along_x, along_y):
        inside = (along_x >= tx * CX) & (along_x < tx * CX + CX)
        inside = inside & (along_y >= ty * CY) & (along_y < ty * CY + CY)
        return jnp.where(inside, (along_x - tx * CX) * CY + along_y - ty * CY, -1)

    source_row = local_row(source_s[0, 0], source_s[0, 1])
    cell_row = local_row(cell_v[0:1, :], cell_v[1:2, :])
    injected = jnp.where(row == source_row, strength_s[0], 0.0)
    recorded = jnp.sum(
        jnp.where(jnp.broadcast_to(row, (ROWS, NREC)) == cell_row, trace_v[...], 0.0),
        axis=1,
        keepdims=True,
    )
    surface = lax.broadcasted_iota(jnp.int32, (ROWS, CZ), 1) == SURFACE_DEPTH

    loads[5].wait()
    loads[6].wait()
    loads[7].wait()
    for n in (2, 3, 0, 1):
        came_from = sides[(1, 0, 3, 2)[n]][0]

        @pl.when(came_from)
        def _():
            halo_copy(n).wait_recv()

    for field, extra in ((0, injected), (1, recorded)):
        layers = halo[field]
        beyond = mm(halo_w[0:ROWS, 0:HALO], layers) + mm(halo_w[ROWS:, 0:HALO], layers)
        beyond = beyond + jnp.where(surface, jnp.broadcast_to(extra, (ROWS, CZ)), 0.0)
        lap[field] = lap[field] + beyond.reshape(CX, CY, CZ)
        prev[field] = 2.0 * now[field] - prev[field]

    table_copy.wait()

    def corr_copy(d):
        owner = lax.rem(me + d, NS)
        return pltpu.make_async_remote_copy(
            src_ref=corr_send.at[owner],
            dst_ref=corr_in.at[me],
            send_sem=c_send.at[d],
            recv_sem=c_recv.at[d],
            device_id={"shot": owner},
            device_id_type=MESH,
        )

    def contribute(owner):
        pair = arrived[owner].astype(jnp.float32)
        products = []
        for k in range(2):
            scaled = pair[k * CY : (k + 1) * CY] * STEP_RATIO
            courant = scaled * scaled
            speed[2 * owner + k] = courant
            r = smem_tables[1, 0, 2 * owner + k]
            products.append(
                (prev[0, r] + courant * lap[0, r]) * (prev[1, r] + courant * lap[1, r])
            )
        both = jnp.concatenate(products, axis=0)
        top = both.astype(jnp.bfloat16)
        return top, (both - top.astype(jnp.float32)).astype(jnp.bfloat16)

    corr_in[me, 0], corr_in[me, 1] = contribute(me)

    @pl.loop(1, NS)
    def _(d):
        block_copy(d).wait_recv()
        owner = lax.rem(me + d, NS)
        corr_send[owner, 0], corr_send[owner, 1] = contribute(owner)
        corr_copy(d).start()

    @pl.loop(0, CX)
    def _(r):
        courant = speed[smem_tables[0, 0, r]]
        for field in range(2):
            prev[field, r] = prev[field, r] + courant * lap[field, r]

    outs = [
        pltpu.make_async_copy(prev.at[0], f_out.at[0], out_sem.at[0]),
        pltpu.make_async_copy(prev.at[1], a_out.at[0], out_sem.at[1]),
        pltpu.make_async_copy(image, image_out.at[0], out_sem.at[2]),
    ]
    outs[0].start()
    outs[1].start()
    chosen = hit[...].T.astype(jnp.bfloat16)

    @pl.loop(1, NS)
    def _(d):
        corr_copy(d).wait_recv()

    tops = corr_in[:, 0].reshape(ROWS, CZ)
    rests = corr_in[:, 1].reshape(ROWS, CZ)
    image[...] = (mm(chosen, tops) + mm(chosen, rests)).reshape(SLAB, CY, CZ)
    outs[2].start()

    @pl.loop(1, NS)
    def _(d):
        id_copy(d).wait_send()
        block_copy(d).wait_send()
        corr_copy(d).wait_send()

    for n in range(4):

        @pl.when(sides[n][0])
        def _():
            halo_copy(n).wait_send()

    for out in outs:
        out.wait()


def on_device(*arrays):
    arrays = arrays[:8] + (jnp.swapaxes(arrays[8], 1, 2),) + arrays[9:]
    square, halo_w = stencil_constants()
    field = jax.ShapeDtypeStruct((1, CX, CY, CZ), jnp.float32)
    dma = pltpu.SemaphoreType.DMA
    bf, f32, i32 = jnp.bfloat16, jnp.float32, jnp.int32
    scratch = [
        pltpu.VMEM((2, CX, CY, CZ), f32),
        pltpu.VMEM((2, CX, CY, CZ), f32),
        pltpu.VMEM((2, CX, CY, CZ), f32),
        pltpu.VMEM((2, ROWS, CZ), bf),
        pltpu.VMEM((2, ROWS, CZ), bf),
        pltpu.VMEM((SLAB, CY, CZ), bf),
        pltpu.VMEM((SLAB, CY, CZ), f32),
        pltpu.VMEM((1, CX), i32),
        pltpu.VMEM((2, NREC), i32),
        pltpu.VMEM((1, NREC), f32),
        pltpu.VMEM(square.shape, bf),
        pltpu.VMEM(halo_w.shape, bf),
        pltpu.VMEM((2, 2, YH, CZ), bf),
        pltpu.VMEM((2, HALO, CZ), bf),
        pltpu.VMEM((2, 1, 128), i32),
        pltpu.VMEM((1, 128), i32),
        pltpu.VMEM((NS, 1, 128), i32),
        pltpu.SMEM((NS, 1, 128), i32),
        pltpu.VMEM((NS, 2 * CY, CZ), bf),
        pltpu.VMEM((NS, 2 * CY, CZ), bf),
        pltpu.VMEM((2 * NS, CY, CZ), f32),
        pltpu.VMEM((NS, 2, 2 * CY, CZ), bf),
        pltpu.VMEM((NS, 2, 2 * CY, CZ), bf),
        pltpu.VMEM((ROWS, ROWS), f32),
        pltpu.VMEM((SLAB, CY, CZ), f32),
        pltpu.SMEM((2, 1, 128), i32),
        pltpu.SMEM((1, 2), i32),
        pltpu.SMEM((1,), f32),
        dma((12,)),
        dma((2,)),
        dma((NS,)),
        dma((NS,)),
        dma((4,)),
        dma((4,)),
        dma((NS,)),
        dma((NS,)),
        dma((NS,)),
        dma((NS,)),
        dma((3,)),
    ]
    anywhere = pl.BlockSpec(memory_space=pl.ANY)
    hbm = pl.BlockSpec(memory_space=pltpu.HBM)
    return pl.pallas_call(
        kernel,
        out_shape=(field, field, field),
        in_specs=[hbm] * 12,
        out_specs=(anywhere,) * 3,
        scratch_shapes=scratch,
        compiler_params=pltpu.CompilerParams(
            collective_id=0, has_side_effects=True, vmem_limit_bytes=64 * 1024 * 1024
        ),
    )(*arrays, jnp.asarray(square), jnp.asarray(halo_w))


def solution(mesh):
    in_specs = (
        P("shot", "tx", "ty", None),
        P("shot", "tx", "ty", None),
        P("shot", "tx", "ty", None),
        P("shot", "tx", "ty", None),
        P(("tx", "ty"), "shot", None, None),
        P("shot", ("tx", "ty"), None),
        P("shot", None),
        P("shot"),
        P("shot", None, None),
        P("shot", None),
    )
    out_specs = (
        P("shot", "tx", "ty", None),
        P("shot", "tx", "ty", None),
        P(("tx", "ty"), "shot", None, None),
    )
    return jax.shard_map(
        on_device, mesh=mesh, in_specs=in_specs, out_specs=out_specs, check_vma=False
    )
```

time: 167 us -> 42.1 us (0.25)
  waiting for transfers between devices: 91.9 us -> 0 us
  Pallas kernels: 0 us -> 37.1 us
  starting transfers between devices: 37.1 us -> 0 us
  between operations: 15 us -> 1.3 us
  local copies, waits for them, and re-layouts: 10.8 us -> 3.46 us
  other arithmetic: 5.52 us -> 0 us
  matrix products: 5.42 us -> 0 us
    reduce_scatter x1 -> x0, waiting for transfers between devices: 87.7 us -> none  [on_device(): lax.psum_scatter(jnp.dot(matches, correlation, precision=lax.Precision.HI...]
    pallas_call x0 -> x1, Pallas kernels: none -> 37.1 us  [on_device(): pl.pallas_call(kernel, out_shape=(field, field, field), in_specs=[hbm] *...]
    ppermute x4 -> x0, starting transfers between devices: 24.1 us -> none  [the longest x2 14 us: padded_2(): lax.ppermute(tail, axis, [(i, (i + 1) % count) for i in range(ends)])]
    all_to_all x2 -> x0, starting transfers between devices: 13 us -> none  [the longest x1 6.75 us: on_device(): lax.all_to_all(wanted.reshape(shot_count, capacity), 'shot', split_axis=0...]
    dot_general x4 -> x0, matrix products: 5.42 us -> none  [the longest x1 3.74 us: on_device(): jnp.dot(matches, correlation, precision=lax.Precision.HIGHEST)]
    ppermute x4 -> x0, waiting for transfers between devices: 2.76 us -> none  [the longest x2 1.48 us: padded_2(): lax.ppermute(tail, axis, [(i, (i + 1) % count) for i in range(ends)])]
    unnamed x15 -> x7, local copies, waits for them, and re-layouts: 5.52 us -> 3.46 us
  transfers between devices with their start and end apart: 7 -> 0, of which waited for: 5 -> 0; matrix products, arithmetic and copies ran while one was open for 7% -> 0% of each run, Pallas kernels for 0% -> 0%
where the time goes in v1:
time: 42.1 us; the launch traced here: 41.9 us
  Pallas kernels  37.1 us (88%)
  local copies, waits for them, and re-layouts  3.46 us (8%)
  between operations  1.3 us (3%)
    pallas_call x1, Pallas kernels, on_device(): pl.pallas_call(kernel, out_shape=(field, field, field), in_specs=[hbm] *...  37.1 us
    unnamed x7, local copies, waits for them, and re-layouts  3.46 us

profile of v1, /device:TPU:1, one launch (start us, length us, event | category | flops | bytes accessed | tf_op | source)
XLA Modules:
  0.0 41.9 jit_solution(6877751035408654449)
XLA Ops:
  1.3 37.1 %shard_map.139 = (f32[1,32,8,256]{3,2,1,0:T(8,128)}, f32[1,32,8,256]{3,2,1,0:T(8,128)}, f32[1,32,8,256]{3,2,1,0:T(8,128)}) custom-call(f32[1,32,8,256]{3,2,1,0:T(8,128)} %f_prev.1, f32[1,32,8,256]{3,2,1,0:T(8,128)} %f_now.1, f32[1,32,8,256]{3,2,1,0:T(8,128)} %a_prev.1, f32[1,32,8,256]{3,2,1,0:T(8,128)} %a_now.1, bf16[1,32,8,256]{3,2,1,0:T(8,128)(2,1)} %velocity.1, ...), custom_call_target="tpu_custom_call" | custom-call | tf_op jit(solution)/shard_map/pallas_call | solution.py:413
  38.4 0.0 copy-start.1
  38.4 1.7 %copy.19 = f32[1,32,8,256]{3,2,1,0:T(8,128)} copy(f32[1,32,8,256]{3,2,1,0:T(8,128)} %get-tuple-element.6) | data formatting | bytes 524288
  40.1 0.0 copy-done.1
  40.1 0.0 copy-start
  40.1 0.7 %copy.20 = f32[1,32,8,256]{3,2,1,0:T(8,128)} copy(f32[1,32,8,256]{3,2,1,0:T(8,128)S(1)} %copy-done.1) | data formatting | bytes 524288
  40.8 0.3 copy-done
  41.2 0.7 %copy.21 = f32[1,32,8,256]{3,2,1,0:T(8,128)} copy(f32[1,32,8,256]{3,2,1,0:T(8,128)S(1)} %copy-done) | data formatting | bytes 524288
Async XLA Ops:
  38.4 1.7 %copy-start.1 = (f32[1,32,8,256]{3,2,1,0:T(8,128)S(1)}, f32[1,32,8,256]{3,2,1,0:T(8,128)}, u32[]{:S(2)}) copy-start(f32[1,32,8,256]{3,2,1,0:T(8,128)} %get-tuple-element.7) | copy-start | bytes 786436
  40.1 1.0 %copy-start = (f32[1,32,8,256]{3,2,1,0:T(8,128)S(1)}, f32[1,32,8,256]{3,2,1,0:T(8,128)}, u32[]{:S(2)}) copy-start(f32[1,32,8,256]{3,2,1,0:T(8,128)} %get-tuple-element.8) | copy-start | bytes 786436

commit v2 on v1

--- a/solution.py
+++ b/solution.py
@@ -21,6 +21,8 @@
 YH = CX * 4
 XH = 4 * CY
 HALO = 2 * YH + 2 * XH
+AHEAD = 4
+LIMIT = 62 * 1024 * 1024
 
 
 def stencil_constants():
@@ -64,13 +66,13 @@
 def kernel(
     f_prev, f_now, a_prev, a_now, velocity, aperture, source_cell, strength, receivers, traces,
     square_hbm, halo_hbm,
-    f_out, a_out, image_out,
-    now, prev, lap, high, low, slab_b, slab, ids, cell_v, trace_v, square, halo_w,
-    pick_send, halo, tables, wanted, wanted_v, wanted_by, blocks, arrived, speed, corr_send, corr_in,
-    hit, image,
+    prev, corr_in, hit_out,
+    now, lap, high, low, slab_b, slab, ids, cell_v, trace_v, square, halo_w,
+    pick_send, halo, tables, wanted, wanted_v, wanted_by, blocks, arrived, speed, corr_send,
+    hit,
     smem_tables, source_s, strength_s,
-    load_sem, table_sem, id_send, id_recv, halo_send, halo_recv, v_send, v_recv, c_send, c_recv,
-    out_sem,
+    load_sem, table_sem, id_sem, id_send, id_recv, halo_send, halo_recv, v_send, v_recv,
+    c_send, c_recv, ready,
 ):
     me = lax.axis_index("shot")
     tx = lax.axis_index("tx")
@@ -101,16 +103,20 @@
             barrier, inc=1, device_id={"shot": lax.rem(me + d, NS)}, device_id_type=MESH
         )
 
+    odd = lax.rem(tx, 2) == 1
     sides = [
         (ty < NTY - 1, "ty", ty + 1),
         (ty > 0, "ty", ty - 1),
         (tx < NTX - 1, "tx", tx + 1),
         (tx > 0, "tx", tx - 1),
     ]
-    for present, axis, other in sides:
-
-        @pl.when(present)
-        def _():
+    first = [ty < NTY - 1, None, odd & (tx < NTX - 1), odd & (tx > 0)]
+    second = [None, ty > 0, jnp.logical_not(odd) & (tx < NTX - 1), jnp.logical_not(odd) & (tx > 0)]
+    for n in (0, 2, 3):
+
+        @pl.when(first[n])
+        def _():
+            axis, other = sides[n][1:]
             pl.semaphore_signal(barrier, inc=1, device_id={axis: other}, device_id_type=MESH)
 
     for present, start, size in (
@@ -153,14 +159,19 @@
         pick_send[0, field] = picked[0:YH]
         pick_send[1, field] = picked[YH:]
 
-    partners = (
-        NS - 1
-        + (ty > 0).astype(jnp.int32)
-        + (ty < NTY - 1).astype(jnp.int32)
-        + (tx > 0).astype(jnp.int32)
-        + (tx < NTX - 1).astype(jnp.int32)
-    )
+    partners = NS - 1
+    for n in (1, 2, 3):
+        partners = partners + second[n].astype(jnp.int32)
     pl.semaphore_wait(barrier, partners)
+
+    for n in (1, 2, 3):
+
+        @pl.when(second[n])
+        def _():
+            axis, other = sides[n][1:]
+            pl.semaphore_signal(
+                ready.at[(1, 0, 3, 2)[n]], inc=1, device_id={axis: other}, device_id_type=MESH
+            )
 
     def id_copy(d):
         return pltpu.make_async_remote_copy(
@@ -192,10 +203,16 @@
             device_id_type=MESH,
         )
 
-    for n in (2, 3, 0, 1):
-
-        @pl.when(sides[n][0])
-        def _():
+    for n in (2, 3, 1):
+
+        @pl.when(second[n])
+        def _():
+            halo_copy(n).start()
+
+    def answer(n):
+        @pl.when(first[n])
+        def _():
+            pl.semaphore_wait(ready.at[n], 1)
             halo_copy(n).start()
 
     loads[4].wait()
@@ -227,15 +244,26 @@
             device_id_type=MESH,
         )
 
-    @pl.loop(1, NS)
-    def _(d):
-        id_copy(d).wait_recv()
+    def id_local(d):
         shot = lax.rem(me - d + NS, NS)
-        local = pltpu.make_async_copy(wanted_v.at[shot], wanted_by.at[shot], table_sem.at[1])
-        local.start()
-        local.wait()
-        blocks[shot] = serve(shot)
-        block_copy(d).start()
+        return pltpu.make_async_copy(wanted_v.at[shot], wanted_by.at[shot], id_sem.at[d])
+
+    @pl.loop(1, NS + AHEAD)
+    def _(step):
+        @pl.when(step < NS)
+        def _():
+            id_copy(step).wait_recv()
+            id_local(step).start()
+
+        @pl.when(step > AHEAD)
+        def _():
+            d = step - AHEAD
+            id_local(d).wait()
+            shot = lax.rem(me - d + NS, NS)
+            blocks[shot] = serve(shot)
+            block_copy(d).start()
+
+    answer(0)
 
     for field in range(2):
         top, rest = high[field], low[field]
@@ -270,6 +298,8 @@
     loads[5].wait()
     loads[6].wait()
     loads[7].wait()
+    answer(3)
+    answer(2)
     for n in (2, 3, 0, 1):
         came_from = sides[(1, 0, 3, 2)[n]][0]
 
@@ -327,23 +357,11 @@
         for field in range(2):
             prev[field, r] = prev[field, r] + courant * lap[field, r]
 
-    outs = [
-        pltpu.make_async_copy(prev.at[0], f_out.at[0], out_sem.at[0]),
-        pltpu.make_async_copy(prev.at[1], a_out.at[0], out_sem.at[1]),
-        pltpu.make_async_copy(image, image_out.at[0], out_sem.at[2]),
-    ]
-    outs[0].start()
-    outs[1].start()
-    chosen = hit[...].T.astype(jnp.bfloat16)
+    hit_out[...] = hit[...].T.astype(jnp.bfloat16)
 
     @pl.loop(1, NS)
     def _(d):
         corr_copy(d).wait_recv()
-
-    tops = corr_in[:, 0].reshape(ROWS, CZ)
-    rests = corr_in[:, 1].reshape(ROWS, CZ)
-    image[...] = (mm(chosen, tops) + mm(chosen, rests)).reshape(SLAB, CY, CZ)
-    outs[2].start()
 
     @pl.loop(1, NS)
     def _(d):
@@ -357,6 +375,19 @@
         def _():
             halo_copy(n).wait_send()
 
+
+def finish(values, corr_in, hit, f_out, a_out, image_out, image, out_sem):
+    outs = [
+        pltpu.make_async_copy(values.at[0], f_out.at[0], out_sem.at[0]),
+        pltpu.make_async_copy(values.at[1], a_out.at[0], out_sem.at[1]),
+        pltpu.make_async_copy(image, image_out.at[0], out_sem.at[2]),
+    ]
+    outs[0].start()
+    outs[1].start()
+    tops = corr_in[:, 0].reshape(ROWS, CZ)
+    rests = corr_in[:, 1].reshape(ROWS, CZ)
+    image[...] = (mm(hit[...], tops) + mm(hit[...], rests)).reshape(SLAB, CY, CZ)
+    outs[2].start()
     for out in outs:
         out.wait()
 
@@ -368,7 +399,6 @@
     dma = pltpu.SemaphoreType.DMA
     bf, f32, i32 = jnp.bfloat16, jnp.float32, jnp.int32
     scratch = [
-        pltpu.VMEM((2, CX, CY, CZ), f32),
         pltpu.VMEM((2, CX, CY, CZ), f32),
         pltpu.VMEM((2, CX, CY, CZ), f32),
         pltpu.VMEM((2, ROWS, CZ), bf),
@@ -390,9 +420,7 @@
         pltpu.VMEM((NS, 2 * CY, CZ), bf),
         pltpu.VMEM((2 * NS, CY, CZ), f32),
         pltpu.VMEM((NS, 2, 2 * CY, CZ), bf),
-        pltpu.VMEM((NS, 2, 2 * CY, CZ), bf),
         pltpu.VMEM((ROWS, ROWS), f32),
-        pltpu.VMEM((SLAB, CY, CZ), f32),
         pltpu.SMEM((2, 1, 128), i32),
         pltpu.SMEM((1, 2), i32),
         pltpu.SMEM((1,), f32),
@@ -400,26 +428,39 @@
         dma((2,)),
         dma((NS,)),
         dma((NS,)),
+        dma((NS,)),
         dma((4,)),
         dma((4,)),
         dma((NS,)),
         dma((NS,)),
         dma((NS,)),
         dma((NS,)),
-        dma((3,)),
+        pltpu.SemaphoreType.REGULAR((4,)),
     ]
     anywhere = pl.BlockSpec(memory_space=pl.ANY)
-    hbm = pl.BlockSpec(memory_space=pltpu.HBM)
-    return pl.pallas_call(
+    vmem = pl.BlockSpec(memory_space=pltpu.VMEM)
+    values, corr_in, hit = pl.pallas_call(
         kernel,
-        out_shape=(field, field, field),
-        in_specs=[hbm] * 12,
-        out_specs=(anywhere,) * 3,
+        out_shape=(
+            jax.ShapeDtypeStruct((2, CX, CY, CZ), f32),
+            jax.ShapeDtypeStruct((NS, 2, 2 * CY, CZ), bf),
+            jax.ShapeDtypeStruct((ROWS, ROWS), bf),
+        ),
+        in_specs=[anywhere] * 12,
+        out_specs=(vmem,) * 3,
         scratch_shapes=scratch,
         compiler_params=pltpu.CompilerParams(
-            collective_id=0, has_side_effects=True, vmem_limit_bytes=64 * 1024 * 1024
+            collective_id=0, has_side_effects=True, vmem_limit_bytes=LIMIT
         ),
     )(*arrays, jnp.asarray(square), jnp.asarray(halo_w))
+    return pl.pallas_call(
+        finish,
+        out_shape=(field, field, field),
+        in_specs=[vmem] * 3,
+        out_specs=(anywhere,) * 3,
+        scratch_shapes=[pltpu.VMEM((SLAB, CY, CZ), f32), dma((3,))],
+        compiler_params=pltpu.CompilerParams(vmem_limit_bytes=LIMIT),
+    )(values, corr_in, hit)
 
 
 def solution(mesh):

time: 42.1 us -> 33.2 us (0.79)
  Pallas kernels: 37.1 us -> 31.7 us
  local copies, waits for them, and re-layouts: 3.46 us -> 0 us
    pallas_call x1 -> x2, Pallas kernels: 37.1 us -> 31.7 us  [the longest x1 29.6 us: on_device(): pl.pallas_call(kernel, out_shape=(jax.ShapeDtypeStruct((2, CX, CY, CZ), f...]
    unnamed x7 -> x0, local copies, waits for them, and re-layouts: 3.46 us -> none
where the time goes in v2:
time: 33.2 us; the launch traced here: 33 us
  Pallas kernels  31.7 us (95%)
  between operations  1.29 us (4%)
    pallas_call x1, Pallas kernels, on_device(): pl.pallas_call(kernel, out_shape=(jax.ShapeDtypeStruct((2, CX, CY, CZ), f...  29.6 us
    pallas_call x1, Pallas kernels, on_device(): pl.pallas_call(finish, out_shape=(field, field, field), in_specs=[vmem] *...  2.1 us

profile of v2, /device:TPU:1, one launch (start us, length us, event | category | flops | bytes accessed | tf_op | source)
XLA Modules:
  0.0 33.0 jit_solution(17889802777405615138)
XLA Ops:
  1.3 29.6 %shard_map.139 = (f32[2,32,8,256]{3,2,1,0:T(8,128)}, bf16[16,2,16,256]{3,2,1,0:T(8,128)(2,1)}, bf16[256,256]{1,0:T(8,128)(2,1)}) custom-call(f32[1,32,8,256]{3,2,1,0:T(8,128)} %f_prev.1, f32[1,32,8,256]{3,2,1,0:T(8,128)} %f_now.1, f32[1,32,8,256]{3,2,1,0:T(8,128)} %a_prev.1, f32[1,32,8,256]{3,2,1,0:T(8,128)} %a_now.1, bf16[1,32,8,256]{3,2,1,0:T(8,128)(2,1)} %velocity.1, ...), custom_call_target="tpu_custom_call" | custom-call | tf_op jit(solution)/shard_map/pallas_call | solution.py:442
  30.9 2.1 %shard_map.140 = (f32[1,32,8,256]{3,2,1,0:T(8,128)}, f32[1,32,8,256]{3,2,1,0:T(8,128)}, f32[1,32,8,256]{3,2,1,0:T(8,128)}) custom-call(f32[2,32,8,256]{3,2,1,0:T(8,128)} %get-tuple-element.6.values, bf16[16,2,16,256]{3,2,1,0:T(8,128)(2,1)} %get-tuple-element.7.corr_in, bf16[256,256]{1,0:T(8,128)(2,1)} %get-tuple-element.8.hit), custom_call_target="tpu_custom_call" | custom-call | tf_op jit(solution)/shard_map/pallas_call | solution.py:456

commit v3 on v2

--- a/solution.py
+++ b/solution.py
@@ -21,8 +21,7 @@
 YH = CX * 4
 XH = 4 * CY
 HALO = 2 * YH + 2 * XH
-AHEAD = 4
-LIMIT = 62 * 1024 * 1024
+LIMIT = 40 * 1024 * 1024
 
 
 def stencil_constants():
@@ -72,7 +71,7 @@
     hit,
     smem_tables, source_s, strength_s,
     load_sem, table_sem, id_sem, id_send, id_recv, halo_send, halo_recv, v_send, v_recv,
-    c_send, c_recv, ready,
+    c_send, c_recv, ready, go,
 ):
     me = lax.axis_index("shot")
     tx = lax.axis_index("tx")
@@ -95,14 +94,8 @@
     for load in loads:
         load.start()
 
-    barrier = pltpu.get_barrier_semaphore()
-
-    @pl.loop(1, NS)
-    def _(d):
-        pl.semaphore_signal(
-            barrier, inc=1, device_id={"shot": lax.rem(me + d, NS)}, device_id_type=MESH
-        )
-
+    relayed = tx == 2
+    home = tx + relayed.astype(jnp.int32)
     odd = lax.rem(tx, 2) == 1
     sides = [
         (ty < NTY - 1, "ty", ty + 1),
@@ -110,14 +103,32 @@
         (tx < NTX - 1, "tx", tx + 1),
         (tx > 0, "tx", tx - 1),
     ]
-    first = [ty < NTY - 1, None, odd & (tx < NTX - 1), odd & (tx > 0)]
-    second = [None, ty > 0, jnp.logical_not(odd) & (tx < NTX - 1), jnp.logical_not(odd) & (tx > 0)]
-    for n in (0, 2, 3):
+    first = [ty < NTY - 1, None, tx == 1, tx == 1]
+
+    barrier = pltpu.get_barrier_semaphore()
+
+    @pl.loop(1 - relayed.astype(jnp.int32), NS)
+    def _(d):
+        pl.semaphore_signal(
+            barrier,
+            inc=1,
+            device_id={"shot": lax.rem(me + d, NS), "tx": home},
+            device_id_type=MESH,
+        )
+
+    @pl.when(first[0])
+    def _():
+        pl.semaphore_signal(
+            barrier, inc=1, device_id={"tx": home, "ty": ty + 1}, device_id_type=MESH
+        )
+
+    for n in (2, 3):
 
         @pl.when(first[n])
         def _():
-            axis, other = sides[n][1:]
-            pl.semaphore_signal(barrier, inc=1, device_id={axis: other}, device_id_type=MESH)
+            pl.semaphore_signal(
+                barrier, inc=1, device_id={"tx": sides[n][2]}, device_id_type=MESH
+            )
 
     for present, start, size in (
         (ty > 0, 0, YH),
@@ -129,6 +140,41 @@
         @pl.when(jnp.logical_not(present))
         def _():
             halo[:, start : start + size, :] = jnp.zeros((2, size, CZ), jnp.bfloat16)
+
+    for field in range(2):
+        loads[1 + field].wait()
+        u = now[field].reshape(ROWS, CZ)
+        top = u.astype(jnp.bfloat16)
+        high[field] = top
+        low[field] = (u - top.astype(jnp.float32)).astype(jnp.bfloat16)
+
+    def halo_copy(n):
+        axis, other = sides[n][1], sides[n][2]
+        start = (0, YH, 2 * YH, 2 * YH + XH)[n]
+        if n < 2:
+            source, size = pick_send.at[n], YH
+        else:
+            source, size = high.at[:, pl.ds((CX - 4) * CY if n == 2 else 0, XH)], XH
+        return pltpu.make_async_remote_copy(
+            src_ref=source,
+            dst_ref=halo.at[:, pl.ds(start, size)],
+            send_sem=halo_send.at[n],
+            recv_sem=halo_recv.at[n],
+            device_id={axis: other},
+            device_id_type=MESH,
+        )
+
+    def answer_first(n):
+        axis, other = sides[n][1:]
+        pl.semaphore_signal(
+            ready.at[(1, 0, 3, 2)[n]], inc=1, device_id={axis: other}, device_id_type=MESH
+        )
+
+    @pl.when(relayed)
+    def _():
+        pl.semaphore_wait(barrier, 1)
+        answer_first(3)
+        halo_copy(3).start()
 
     loads[0].wait()
     row_l = lax.broadcasted_iota(jnp.int32, (CX, CX), 1)
@@ -147,31 +193,26 @@
     own_copy = pltpu.make_async_copy(wanted, wanted_by.at[me], table_sem.at[1])
     own_copy.start()
 
-    for field in range(2):
-        loads[1 + field].wait()
-        u = now[field].reshape(ROWS, CZ)
-        top = u.astype(jnp.bfloat16)
-        high[field] = top
-        low[field] = (u - top.astype(jnp.float32)).astype(jnp.bfloat16)
     loads[3].wait()
     for field in range(2):
         picked = mm(square[4 * ROWS : 5 * ROWS, :], high[field]).astype(jnp.bfloat16)
         pick_send[0, field] = picked[0:YH]
         pick_send[1, field] = picked[YH:]
 
-    partners = NS - 1
-    for n in (1, 2, 3):
-        partners = partners + second[n].astype(jnp.int32)
-    pl.semaphore_wait(barrier, partners)
-
-    for n in (1, 2, 3):
-
-        @pl.when(second[n])
-        def _():
-            axis, other = sides[n][1:]
-            pl.semaphore_signal(
-                ready.at[(1, 0, 3, 2)[n]], inc=1, device_id={axis: other}, device_id_type=MESH
-            )
+    partners = NS - 1 + (ty > 0).astype(jnp.int32) + (tx == 0).astype(jnp.int32)
+    partners = partners + jnp.where(tx == 3, NS + (ty > 0).astype(jnp.int32), 0)
+
+    @pl.when(jnp.logical_not(relayed))
+    def _():
+        pl.semaphore_wait(barrier, partners)
+
+    @pl.when(tx == 3)
+    def _():
+        pl.semaphore_signal(go, inc=1, device_id={"tx": 2}, device_id_type=MESH)
+
+    @pl.when(relayed)
+    def _():
+        pl.semaphore_wait(go, 1)
 
     def id_copy(d):
         return pltpu.make_async_remote_copy(
@@ -187,27 +228,25 @@
     def _(d):
         id_copy(d).start()
 
-    def halo_copy(n):
-        axis, other = sides[n][1], sides[n][2]
-        start = (0, YH, 2 * YH, 2 * YH + XH)[n]
-        if n < 2:
-            source, size = pick_send.at[n], YH
-        else:
-            source, size = high.at[:, pl.ds((CX - 4) * CY if n == 2 else 0, XH)], XH
-        return pltpu.make_async_remote_copy(
-            src_ref=source,
-            dst_ref=halo.at[:, pl.ds(start, size)],
-            send_sem=halo_send.at[n],
-            recv_sem=halo_recv.at[n],
-            device_id={axis: other},
-            device_id_type=MESH,
-        )
-
-    for n in (2, 3, 1):
-
-        @pl.when(second[n])
-        def _():
-            halo_copy(n).start()
+    @pl.when(ty > 0)
+    def _():
+        answer_first(1)
+
+    @pl.when(tx == 0)
+    def _():
+        answer_first(2)
+
+    @pl.when(jnp.logical_not(odd))
+    def _():
+        halo_copy(2).start()
+
+    @pl.when(tx == 3)
+    def _():
+        halo_copy(3).start()
+
+    @pl.when(ty > 0)
+    def _():
+        halo_copy(1).start()
 
     def answer(n):
         @pl.when(first[n])
@@ -248,20 +287,17 @@
         shot = lax.rem(me - d + NS, NS)
         return pltpu.make_async_copy(wanted_v.at[shot], wanted_by.at[shot], id_sem.at[d])
 
-    @pl.loop(1, NS + AHEAD)
-    def _(step):
-        @pl.when(step < NS)
-        def _():
-            id_copy(step).wait_recv()
-            id_local(step).start()
-
-        @pl.when(step > AHEAD)
-        def _():
-            d = step - AHEAD
-            id_local(d).wait()
-            shot = lax.rem(me - d + NS, NS)
-            blocks[shot] = serve(shot)
-            block_copy(d).start()
+    @pl.loop(1, NS)
+    def _(d):
+        id_copy(d).wait_recv()
+        id_local(d).start()
+
+    @pl.loop(1, NS)
+    def _(d):
+        id_local(d).wait()
+        shot = lax.rem(me - d + NS, NS)
+        blocks[shot] = serve(shot)
+        block_copy(d).start()
 
     answer(0)
 
@@ -287,7 +323,7 @@
 
     source_row = local_row(source_s[0, 0], source_s[0, 1])
     cell_row = local_row(cell_v[0:1, :], cell_v[1:2, :])
-    injected = jnp.where(row == source_row, strength_s[0], 0.0)
+    injected = jnp.where(row == source_row, strength_s[0, 0], 0.0)
     recorded = jnp.sum(
         jnp.where(jnp.broadcast_to(row, (ROWS, NREC)) == cell_row, trace_v[...], 0.0),
         axis=1,
@@ -393,8 +429,15 @@
 
 
 def on_device(*arrays):
-    arrays = arrays[:8] + (jnp.swapaxes(arrays[8], 1, 2),) + arrays[9:]
     square, halo_w = stencil_constants()
+    arrays = (
+        *arrays[:7],
+        arrays[7].reshape(1, 1),
+        jnp.swapaxes(arrays[8], 1, 2),
+        arrays[9],
+        jnp.asarray(square),
+        jnp.asarray(halo_w),
+    )
     field = jax.ShapeDtypeStruct((1, CX, CY, CZ), jnp.float32)
     dma = pltpu.SemaphoreType.DMA
     bf, f32, i32 = jnp.bfloat16, jnp.float32, jnp.int32
@@ -423,7 +466,7 @@
         pltpu.VMEM((ROWS, ROWS), f32),
         pltpu.SMEM((2, 1, 128), i32),
         pltpu.SMEM((1, 2), i32),
-        pltpu.SMEM((1,), f32),
+        pltpu.SMEM((1, 1), f32),
         dma((12,)),
         dma((2,)),
         dma((NS,)),
@@ -436,6 +479,7 @@
         dma((NS,)),
         dma((NS,)),
         pltpu.SemaphoreType.REGULAR((4,)),
+        pltpu.SemaphoreType.REGULAR,
     ]
     anywhere = pl.BlockSpec(memory_space=pl.ANY)
     vmem = pl.BlockSpec(memory_space=pltpu.VMEM)
@@ -452,7 +496,7 @@
         compiler_params=pltpu.CompilerParams(
             collective_id=0, has_side_effects=True, vmem_limit_bytes=LIMIT
         ),
-    )(*arrays, jnp.asarray(square), jnp.asarray(halo_w))
+    )(*[a if a.size == 1 else pltpu.with_memory_space_constraint(a, pltpu.HBM) for a in arrays])
     return pl.pallas_call(
         finish,
         out_shape=(field, field, field),

time: 33.2 us -> 29.9 us (0.901)
  Pallas kernels: 31.7 us -> 28.4 us
    pallas_call x1, Pallas kernels: 29.6 us -> 27.5 us  [on_device(): pl.pallas_call(kernel, out_shape=(jax.ShapeDtypeStruct((2, CX, CY, CZ), f...]
    pallas_call x1, Pallas kernels: 2.1 us -> 0.96 us  [on_device(): pl.pallas_call(finish, out_shape=(field, field, field), in_specs=[vmem] *...]
where the time goes in v3:
time: 29.9 us; the launch traced here: 29.7 us
  Pallas kernels  28.4 us (95%)
  between operations  1.29 us (4%)
    pallas_call x1, Pallas kernels, on_device(): pl.pallas_call(kernel, out_shape=(jax.ShapeDtypeStruct((2, CX, CY, CZ), f...  27.5 us
    pallas_call x1, Pallas kernels, on_device(): pl.pallas_call(finish, out_shape=(field, field, field), in_specs=[vmem] *...  0.96 us

profile of v3, /device:TPU:1, one launch (start us, length us, event | category | flops | bytes accessed | tf_op | source)
XLA Modules:
  0.0 29.7 jit_solution(3886248777054899289)
XLA Ops:
  1.3 27.5 %shard_map.139 = (f32[2,32,8,256]{3,2,1,0:T(8,128)S(1)}, bf16[16,2,16,256]{3,2,1,0:T(8,128)(2,1)S(1)}, bf16[256,256]{1,0:T(8,128)(2,1)S(1)}) custom-call(f32[1,32,8,256]{3,2,1,0:T(8,128)} %f_prev.1, f32[1,32,8,256]{3,2,1,0:T(8,128)} %f_now.1, f32[1,32,8,256]{3,2,1,0:T(8,128)} %a_prev.1, f32[1,32,8,256]{3,2,1,0:T(8,128)} %a_now.1, ...), custom_call_target="tpu_custom_call" | custom-call | tf_op jit(solution)/shard_map/pallas_call | solution.py:486
  28.8 1.0 %shard_map.140 = (f32[1,32,8,256]{3,2,1,0:T(8,128)}, f32[1,32,8,256]{3,2,1,0:T(8,128)}, f32[1,32,8,256]{3,2,1,0:T(8,128)}) custom-call(f32[2,32,8,256]{3,2,1,0:T(8,128)S(1)} %get-tuple-element.6.values, bf16[16,2,16,256]{3,2,1,0:T(8,128)(2,1)S(1)} %get-tuple-element.7.corr_in, bf16[256,256]{1,0:T(8,128)(2,1)S(1)} %get-tuple-element.8.hit), custom_call_target="tpu_custom_call" | custom-call | tf_op jit(solution)/shard_map/pallas_call | solution.py:500

commit v4 on v3

--- a/solution.py
+++ b/solution.py
@@ -35,7 +35,7 @@
     z = np.arange(CZ)
     depth = band[np.abs(z[:, None] - z[None, :])]
     pick = np.zeros((ROWS, ROWS))
-    halo = np.zeros((ROWS, 384))
+    halo = np.zeros((ROWS, 2 * YH))
     for cx in range(CX):
         for q in range(4):
             pick[cx * 4 + q, cx * CY + CY - 4 + q] = 1.0
@@ -43,11 +43,6 @@
             for cy in range(CY):
                 halo[cx * CY + cy, cx * 4 + q] = band[cy + 4 - q]
                 halo[cx * CY + cy, YH + cx * 4 + q] = band[CY + q - cy]
-    for q in range(4):
-        for cx in range(CX):
-            for cy in range(CY):
-                halo[cx * CY + cy, 2 * YH + q * CY + cy] = band[cx + 4 - q]
-                halo[cx * CY + cy, 2 * YH + XH + q * CY + cy] = band[CX + q - cx]
 
     def parts(matrix):
         high = matrix.astype(np.float32).astype(ml_dtypes.bfloat16)
@@ -66,8 +61,8 @@
     f_prev, f_now, a_prev, a_now, velocity, aperture, source_cell, strength, receivers, traces,
     square_hbm, halo_hbm,
     prev, corr_in, hit_out,
-    now, lap, high, low, slab_b, slab, ids, cell_v, trace_v, square, halo_w,
-    pick_send, halo, tables, wanted, wanted_v, wanted_by, blocks, arrived, speed, corr_send,
+    now, lap, high, low, edge, slab_b, slab, ids, cell_v, trace_v, square, halo_w,
+    pick_send, halo, tables, wanted, wanted_by, blocks, arrived, speed, corr_send,
     hit,
     smem_tables, source_s, strength_s,
     load_sem, table_sem, id_sem, id_send, id_recv, halo_send, halo_recv, v_send, v_recv,
@@ -91,8 +86,8 @@
         pltpu.make_async_copy(source_cell, source_s, load_sem.at[10]),
         pltpu.make_async_copy(strength, strength_s, load_sem.at[11]),
     ]
-    for load in loads:
-        load.start()
+    for n in (0, 1, 2, 4):
+        loads[n].start()
 
     relayed = tx == 2
     home = tx + relayed.astype(jnp.int32)
@@ -130,6 +125,9 @@
                 barrier, inc=1, device_id={"tx": sides[n][2]}, device_id_type=MESH
             )
 
+    for n in (3, 5, 6, 7, 8, 9, 10, 11):
+        loads[n].start()
+
     for present, start, size in (
         (ty > 0, 0, YH),
         (ty < NTY - 1, YH, YH),
@@ -141,20 +139,14 @@
         def _():
             halo[:, start : start + size, :] = jnp.zeros((2, size, CZ), jnp.bfloat16)
 
-    for field in range(2):
-        loads[1 + field].wait()
-        u = now[field].reshape(ROWS, CZ)
-        top = u.astype(jnp.bfloat16)
-        high[field] = top
-        low[field] = (u - top.astype(jnp.float32)).astype(jnp.bfloat16)
-
-    def halo_copy(n):
+    def halo_copy(n, source=None):
         axis, other = sides[n][1], sides[n][2]
         start = (0, YH, 2 * YH, 2 * YH + XH)[n]
-        if n < 2:
-            source, size = pick_send.at[n], YH
-        else:
-            source, size = high.at[:, pl.ds((CX - 4) * CY if n == 2 else 0, XH)], XH
+        size = YH if n < 2 else XH
+        if source is None and n < 2:
+            source = pick_send.at[n]
+        elif source is None:
+            source = high.at[:, pl.ds((CX - 4) * CY if n == 2 else 0, XH)]
         return pltpu.make_async_remote_copy(
             src_ref=source,
             dst_ref=halo.at[:, pl.ds(start, size)],
@@ -170,11 +162,27 @@
             ready.at[(1, 0, 3, 2)[n]], inc=1, device_id={axis: other}, device_id_type=MESH
         )
 
-    @pl.when(relayed)
-    def _():
+    def across():
         pl.semaphore_wait(barrier, 1)
         answer_first(3)
-        halo_copy(3).start()
+        halo_copy(3, edge).start()
+
+    loads[1].wait()
+    loads[2].wait()
+
+    @pl.when(relayed)
+    def _():
+        edge[...] = now[:, 0:4].reshape(2, XH, CZ).astype(jnp.bfloat16)
+
+    @pl.when(relayed & (ty < 6))
+    def _():
+        across()
+
+    for field in range(2):
+        u = now[field].reshape(ROWS, CZ)
+        top = u.astype(jnp.bfloat16)
+        high[field] = top
+        low[field] = (u - top.astype(jnp.float32)).astype(jnp.bfloat16)
 
     loads[0].wait()
     row_l = lax.broadcasted_iota(jnp.int32, (CX, CX), 1)
@@ -187,11 +195,9 @@
     placed = jnp.broadcast_to(slot, (CX, CX)).T == row_l
     tables[0, :, 0:CX] = slot
     tables[1, :, 0:CX] = jnp.sum(jnp.where(placed, row_s, 0), axis=0, keepdims=True)
-    wanted[:, 0:CX] = jnp.sum(jnp.where(placed, ids_s & (SLAB - 1), 0), axis=0, keepdims=True)
-    table_copy = pltpu.make_async_copy(tables, smem_tables, table_sem.at[0])
+    wanted[me, :, 0:CX] = jnp.sum(jnp.where(placed, ids_s & (SLAB - 1), 0), axis=0, keepdims=True)
+    table_copy = pltpu.make_async_copy(tables, smem_tables, table_sem)
     table_copy.start()
-    own_copy = pltpu.make_async_copy(wanted, wanted_by.at[me], table_sem.at[1])
-    own_copy.start()
 
     loads[3].wait()
     for field in range(2):
@@ -216,10 +222,10 @@
 
     def id_copy(d):
         return pltpu.make_async_remote_copy(
-            src_ref=wanted,
-            dst_ref=wanted_v.at[me],
-            send_sem=id_send.at[d],
-            recv_sem=id_recv.at[d],
+            src_ref=wanted.at[me],
+            dst_ref=wanted.at[me],
+            send_sem=id_send,
+            recv_sem=id_recv,
             device_id={"shot": lax.rem(me + d, NS)},
             device_id_type=MESH,
         )
@@ -227,6 +233,10 @@
     @pl.loop(1, NS)
     def _(d):
         id_copy(d).start()
+
+    @pl.when(relayed & (ty >= 6))
+    def _():
+        across()
 
     @pl.when(ty > 0)
     def _():
@@ -257,7 +267,6 @@
     loads[4].wait()
     slab[...] = slab_b[...].astype(jnp.float32)
 
-    own_copy.wait()
     depth_l = lax.broadcasted_iota(jnp.int32, (CY, ROWS), 1)
     same_y = (depth_l & (CY - 1)) == lax.broadcasted_iota(jnp.int32, (CY, ROWS), 0)
     block_l = jnp.where(same_y, depth_l >> 3, -1)
@@ -270,36 +279,36 @@
         hit[pl.ds(pl.multiple_of(shot * 16, 16), 16), :] = jnp.where(hits, 1.0, 0.0)
         return pair
 
-    arrived[me] = serve(me)
-
     def block_copy(d):
         shot = lax.rem(me - d + NS, NS)
         return pltpu.make_async_remote_copy(
             src_ref=blocks.at[shot],
             dst_ref=arrived.at[me],
-            send_sem=v_send.at[d],
+            send_sem=v_send,
             recv_sem=v_recv.at[d],
             device_id={"shot": shot},
             device_id_type=MESH,
         )
 
-    def id_local(d):
-        shot = lax.rem(me - d + NS, NS)
-        return pltpu.make_async_copy(wanted_v.at[shot], wanted_by.at[shot], id_sem.at[d])
+    all_but_one = pl.ds(0, NS - 1)
+    pltpu.make_async_copy(wanted.at[all_but_one], wanted.at[all_but_one], id_recv).wait()
+    id_local = pltpu.make_async_copy(wanted, wanted_by, id_sem)
+    id_local.start()
+    id_local.wait()
 
     @pl.loop(1, NS)
     def _(d):
-        id_copy(d).wait_recv()
-        id_local(d).start()
-
-    @pl.loop(1, NS)
-    def _(d):
-        id_local(d).wait()
         shot = lax.rem(me - d + NS, NS)
         blocks[shot] = serve(shot)
         block_copy(d).start()
 
+    arrived[me] = serve(me)
     answer(0)
+
+    @pl.when(ty >= 5)
+    def _():
+        answer(3)
+        answer(2)
 
     for field in range(2):
         top, rest = high[field], low[field]
@@ -334,21 +343,37 @@
     loads[5].wait()
     loads[6].wait()
     loads[7].wait()
-    answer(3)
-    answer(2)
-    for n in (2, 3, 0, 1):
-        came_from = sides[(1, 0, 3, 2)[n]][0]
-
-        @pl.when(came_from)
+    def halo_wait(n):
+        @pl.when(sides[(1, 0, 3, 2)[n]][0])
         def _():
             halo_copy(n).wait_recv()
 
+    halo_wait(0)
+    halo_wait(1)
     for field, extra in ((0, injected), (1, recorded)):
-        layers = halo[field]
-        beyond = mm(halo_w[0:ROWS, 0:HALO], layers) + mm(halo_w[ROWS:, 0:HALO], layers)
+        layers = halo[field, 0 : 2 * YH]
+        beyond = mm(halo_w[0:ROWS, :], layers) + mm(halo_w[ROWS:, :], layers)
         beyond = beyond + jnp.where(surface, jnp.broadcast_to(extra, (ROWS, CZ)), 0.0)
         lap[field] = lap[field] + beyond.reshape(CX, CY, CZ)
         prev[field] = 2.0 * now[field] - prev[field]
+
+    @pl.when(ty < 5)
+    def _():
+        answer(3)
+        answer(2)
+
+    halo_wait(2)
+    halo_wait(3)
+    for field in range(2):
+        layers = halo[field, 2 * YH :].astype(jnp.float32).reshape(8, CY, CZ)
+        for q in range(4):
+            for x in range(4):
+                if x <= q:
+                    weight = STENCIL_WEIGHTS[x + 4 - q]
+                    lap[field, x] = lap[field, x] + weight * layers[q]
+                if x >= q:
+                    weight = STENCIL_WEIGHTS[4 + q - x]
+                    lap[field, CX - 4 + x] = lap[field, CX - 4 + x] + weight * layers[4 + q]
 
     table_copy.wait()
 
@@ -357,8 +382,8 @@
         return pltpu.make_async_remote_copy(
             src_ref=corr_send.at[owner],
             dst_ref=corr_in.at[me],
-            send_sem=c_send.at[d],
-            recv_sem=c_recv.at[d],
+            send_sem=c_send,
+            recv_sem=c_recv,
             device_id={"shot": owner},
             device_id_type=MESH,
         )
@@ -395,21 +420,19 @@
 
     hit_out[...] = hit[...].T.astype(jnp.bfloat16)
 
-    @pl.loop(1, NS)
-    def _(d):
-        corr_copy(d).wait_recv()
-
-    @pl.loop(1, NS)
-    def _(d):
-        id_copy(d).wait_send()
-        block_copy(d).wait_send()
-        corr_copy(d).wait_send()
-
+    def all_sent(ref, sem):
+        pltpu.make_async_copy(ref.at[all_but_one], ref.at[all_but_one], sem).wait()
+
+    all_sent(wanted, id_send)
+    all_sent(blocks, v_send)
     for n in range(4):
 
         @pl.when(sides[n][0])
         def _():
             halo_copy(n).wait_send()
+
+    all_sent(corr_send, c_send)
+    all_sent(corr_in, c_recv)
 
 
 def finish(values, corr_in, hit, f_out, a_out, image_out, image, out_sem):
@@ -446,6 +469,7 @@
         pltpu.VMEM((2, CX, CY, CZ), f32),
         pltpu.VMEM((2, ROWS, CZ), bf),
         pltpu.VMEM((2, ROWS, CZ), bf),
+        pltpu.VMEM((2, XH, CZ), bf),
         pltpu.VMEM((SLAB, CY, CZ), bf),
         pltpu.VMEM((SLAB, CY, CZ), f32),
         pltpu.VMEM((1, CX), i32),
@@ -456,7 +480,6 @@
         pltpu.VMEM((2, 2, YH, CZ), bf),
         pltpu.VMEM((2, HALO, CZ), bf),
         pltpu.VMEM((2, 1, 128), i32),
-        pltpu.VMEM((1, 128), i32),
         pltpu.VMEM((NS, 1, 128), i32),
         pltpu.SMEM((NS, 1, 128), i32),
         pltpu.VMEM((NS, 2 * CY, CZ), bf),
@@ -468,16 +491,16 @@
         pltpu.SMEM((1, 2), i32),
         pltpu.SMEM((1, 1), f32),
         dma((12,)),
-        dma((2,)),
-        dma((NS,)),
-        dma((NS,)),
-        dma((NS,)),
+        dma,
+        dma,
+        dma,
+        dma,
         dma((4,)),
         dma((4,)),
+        dma,
         dma((NS,)),
-        dma((NS,)),
-        dma((NS,)),
-        dma((NS,)),
+        dma,
+        dma,
         pltpu.SemaphoreType.REGULAR((4,)),
         pltpu.SemaphoreType.REGULAR,
     ]

time: 29.9 us -> 29.1 us (0.973)
  Pallas kernels: 28.4 us -> 27.7 us
    pallas_call x1, Pallas kernels: 27.5 us -> 26.7 us  [on_device(): pl.pallas_call(kernel, out_shape=(jax.ShapeDtypeStruct((2, CX, CY, CZ), f...]
where the time goes in v4:
time: 29.1 us; the launch traced here: 29 us
  Pallas kernels  27.7 us (95%)
  between operations  1.29 us (4%)
    pallas_call x1, Pallas kernels, on_device(): pl.pallas_call(kernel, out_shape=(jax.ShapeDtypeStruct((2, CX, CY, CZ), f...  26.7 us
    pallas_call x1, Pallas kernels, on_device(): pl.pallas_call(finish, out_shape=(field, field, field), in_specs=[vmem] *...  0.96 us

profile of v4, /device:TPU:1, one launch (start us, length us, event | category | flops | bytes accessed | tf_op | source)
XLA Modules:
  0.0 29.0 jit_solution(9370308389598423250)
XLA Ops:
  1.3 26.7 %shard_map.139 = (f32[2,32,8,256]{3,2,1,0:T(8,128)S(1)}, bf16[16,2,16,256]{3,2,1,0:T(8,128)(2,1)S(1)}, bf16[256,256]{1,0:T(8,128)(2,1)S(1)}) custom-call(f32[1,32,8,256]{3,2,1,0:T(8,128)} %f_prev.1, f32[1,32,8,256]{3,2,1,0:T(8,128)} %f_now.1, f32[1,32,8,256]{3,2,1,0:T(8,128)} %a_prev.1, f32[1,32,8,256]{3,2,1,0:T(8,128)} %a_now.1, ...), custom_call_target="tpu_custom_call" | custom-call | tf_op jit(solution)/shard_map/pallas_call | solution.py:509
  28.0 1.0 %shard_map.140 = (f32[1,32,8,256]{3,2,1,0:T(8,128)}, f32[1,32,8,256]{3,2,1,0:T(8,128)}, f32[1,32,8,256]{3,2,1,0:T(8,128)}) custom-call(f32[2,32,8,256]{3,2,1,0:T(8,128)S(1)} %get-tuple-element.6.values, bf16[16,2,16,256]{3,2,1,0:T(8,128)(2,1)S(1)} %get-tuple-element.7.corr_in, bf16[256,256]{1,0:T(8,128)(2,1)S(1)} %get-tuple-element.8.hit), custom_call_target="tpu_custom_call" | custom-call | tf_op jit(solution)/shard_map/pallas_call | solution.py:523

commit v5 on v4

--- a/solution.py
+++ b/solution.py
@@ -21,6 +21,8 @@
 YH = CX * 4
 XH = 4 * CY
 HALO = 2 * YH + 2 * XH
+STEPS = 32766.0
+TINY = 1e-34
 LIMIT = 40 * 1024 * 1024
 
 
@@ -53,6 +55,12 @@
     return square, np.concatenate(parts(halo), axis=0)
 
 
+def each_partner(body):
+    @pl.loop(1, NS)
+    def _(step):
+        body(lax.rem(5 * step, NS))
+
+
 def mm(a, b):
     return jnp.dot(a, b, preferred_element_type=jnp.float32)
 
@@ -60,12 +68,12 @@
 def kernel(
     f_prev, f_now, a_prev, a_now, velocity, aperture, source_cell, strength, receivers, traces,
     square_hbm, halo_hbm,
-    prev, corr_in, hit_out,
-    now, lap, high, low, edge, slab_b, slab, ids, cell_v, trace_v, square, halo_w,
-    pick_send, halo, tables, wanted, wanted_by, blocks, arrived, speed, corr_send,
+    prev, peak_in, corr_in, hit_out,
+    now, lap, high, low, edge_f, edge, slab_b, slab, ids, cell_v, trace_v, square, halo_w,
+    pick_send, halo, tables, wanted, wanted_by, blocks, arrived, speed, peak_send, corr_send,
     hit,
     smem_tables, source_s, strength_s,
-    load_sem, table_sem, id_sem, id_send, id_recv, halo_send, halo_recv, v_send, v_recv,
+    load_sem, edge_sem, table_sem, id_sem, id_send, id_recv, halo_send, halo_recv, v_send, v_recv,
     c_send, c_recv, ready, go,
 ):
     me = lax.axis_index("shot")
@@ -86,6 +94,16 @@
         pltpu.make_async_copy(source_cell, source_s, load_sem.at[10]),
         pltpu.make_async_copy(strength, strength_s, load_sem.at[11]),
     ]
+    edge_loads = [
+        pltpu.make_async_copy(now_hbm.at[0, 0:4], edge_f.at[field], edge_sem.at[field])
+        for field, now_hbm in enumerate((f_now, a_now))
+    ]
+
+    @pl.when(lax.axis_index("tx") == 2)
+    def _():
+        edge_loads[0].start()
+        edge_loads[1].start()
+
     for n in (0, 1, 2, 4):
         loads[n].start()
 
@@ -167,17 +185,18 @@
         answer_first(3)
         halo_copy(3, edge).start()
 
+    @pl.when(relayed)
+    def _():
+        edge_loads[0].wait()
+        edge_loads[1].wait()
+        edge[...] = edge_f[...].reshape(2, XH, CZ).astype(jnp.bfloat16)
+
+    @pl.when(relayed & (ty < 6))
+    def _():
+        across()
+
     loads[1].wait()
     loads[2].wait()
-
-    @pl.when(relayed)
-    def _():
-        edge[...] = now[:, 0:4].reshape(2, XH, CZ).astype(jnp.bfloat16)
-
-    @pl.when(relayed & (ty < 6))
-    def _():
-        across()
-
     for field in range(2):
         u = now[field].reshape(ROWS, CZ)
         top = u.astype(jnp.bfloat16)
@@ -230,9 +249,7 @@
             device_id_type=MESH,
         )
 
-    @pl.loop(1, NS)
-    def _(d):
-        id_copy(d).start()
+    each_partner(lambda d: id_copy(d).start())
 
     @pl.when(relayed & (ty >= 6))
     def _():
@@ -267,17 +284,9 @@
     loads[4].wait()
     slab[...] = slab_b[...].astype(jnp.float32)
 
-    depth_l = lax.broadcasted_iota(jnp.int32, (CY, ROWS), 1)
-    same_y = (depth_l & (CY - 1)) == lax.broadcasted_iota(jnp.int32, (CY, ROWS), 0)
-    block_l = jnp.where(same_y, depth_l >> 3, -1)
-
     def serve(shot):
-        first = wanted_by[shot, 0, 2 * me]
-        second = wanted_by[shot, 0, 2 * me + 1]
-        pair = jnp.concatenate([slab[first], slab[second]], axis=0).astype(jnp.bfloat16)
-        hits = jnp.concatenate([block_l == first, block_l == second], axis=0)
-        hit[pl.ds(pl.multiple_of(shot * 16, 16), 16), :] = jnp.where(hits, 1.0, 0.0)
-        return pair
+        rows = [slab[wanted_by[shot, 0, 2 * me + k]] for k in range(2)]
+        return jnp.concatenate(rows, axis=0).astype(jnp.bfloat16)
 
     def block_copy(d):
         shot = lax.rem(me - d + NS, NS)
@@ -290,26 +299,6 @@
             device_id_type=MESH,
         )
 
-    all_but_one = pl.ds(0, NS - 1)
-    pltpu.make_async_copy(wanted.at[all_but_one], wanted.at[all_but_one], id_recv).wait()
-    id_local = pltpu.make_async_copy(wanted, wanted_by, id_sem)
-    id_local.start()
-    id_local.wait()
-
-    @pl.loop(1, NS)
-    def _(d):
-        shot = lax.rem(me - d + NS, NS)
-        blocks[shot] = serve(shot)
-        block_copy(d).start()
-
-    arrived[me] = serve(me)
-    answer(0)
-
-    @pl.when(ty >= 5)
-    def _():
-        answer(3)
-        answer(2)
-
     for field in range(2):
         top, rest = high[field], low[field]
         lap[field] = (
@@ -343,6 +332,39 @@
     loads[5].wait()
     loads[6].wait()
     loads[7].wait()
+    all_but_one = pl.ds(0, NS - 1)
+    pltpu.make_async_copy(wanted.at[all_but_one], wanted.at[all_but_one], id_recv).wait()
+    id_local = pltpu.make_async_copy(wanted, wanted_by, id_sem)
+    id_local.start()
+    id_local.wait()
+
+    @each_partner
+    def _(d):
+        shot = lax.rem(me - d + NS, NS)
+        blocks[shot] = serve(shot)
+        block_copy(d).start()
+
+    arrived[me] = serve(me)
+    answer(0)
+
+    @pl.when(ty >= 5)
+    def _():
+        answer(3)
+        answer(2)
+
+    depth_l = lax.broadcasted_iota(jnp.int32, (CY, ROWS), 1)
+    same_y = (depth_l & (CY - 1)) == lax.broadcasted_iota(jnp.int32, (CY, ROWS), 0)
+    block_l = jnp.where(same_y, depth_l >> 3, -1)
+
+
+    @pl.loop(0, NS)
+    def _(shot):
+        hits = [block_l == wanted_by[shot, 0, 2 * me + k] for k in range(2)]
+        rows = pl.ds(pl.multiple_of(shot * 16, 16), 16)
+        hit[rows, :] = jnp.where(jnp.concatenate(hits, axis=0), 1.0, 0.0)
+
+    hit_out[...] = hit[...].T.astype(jnp.bfloat16)
+
     def halo_wait(n):
         @pl.when(sides[(1, 0, 3, 2)[n]][0])
         def _():
@@ -377,16 +399,19 @@
 
     table_copy.wait()
 
-    def corr_copy(d):
+    def corr_copies(d):
         owner = lax.rem(me + d, NS)
-        return pltpu.make_async_remote_copy(
-            src_ref=corr_send.at[owner],
-            dst_ref=corr_in.at[me],
-            send_sem=c_send,
-            recv_sem=c_recv,
-            device_id={"shot": owner},
-            device_id_type=MESH,
-        )
+        return [
+            pltpu.make_async_remote_copy(
+                src_ref=source.at[owner],
+                dst_ref=target.at[me],
+                send_sem=c_send.at[n],
+                recv_sem=c_recv.at[n],
+                device_id={"shot": owner},
+                device_id_type=MESH,
+            )
+            for n, (source, target) in enumerate(((peak_send, peak_in), (corr_send, corr_in)))
+        ]
 
     def contribute(owner):
         pair = arrived[owner].astype(jnp.float32)
@@ -400,17 +425,21 @@
                 (prev[0, r] + courant * lap[0, r]) * (prev[1, r] + courant * lap[1, r])
             )
         both = jnp.concatenate(products, axis=0)
-        top = both.astype(jnp.bfloat16)
-        return top, (both - top.astype(jnp.float32)).astype(jnp.bfloat16)
-
-    corr_in[me, 0], corr_in[me, 1] = contribute(me)
-
-    @pl.loop(1, NS)
+        top = jnp.max(jnp.abs(both), axis=0, keepdims=True)
+        top = jnp.maximum(jnp.maximum(top[:, : CZ // 2], top[:, CZ // 2 :]), TINY)
+        scale = STEPS / top
+        code = jnp.round(both * jnp.concatenate([scale, scale], axis=1))
+        return top, code.astype(jnp.int32).astype(jnp.int16)
+
+    peak_in[me], corr_in[me] = contribute(me)
+
+    @each_partner
     def _(d):
         block_copy(d).wait_recv()
         owner = lax.rem(me + d, NS)
-        corr_send[owner, 0], corr_send[owner, 1] = contribute(owner)
-        corr_copy(d).start()
+        peak_send[owner], corr_send[owner] = contribute(owner)
+        for copy in corr_copies(d):
+            copy.start()
 
     @pl.loop(0, CX)
     def _(r):
@@ -418,8 +447,6 @@
         for field in range(2):
             prev[field, r] = prev[field, r] + courant * lap[field, r]
 
-    hit_out[...] = hit[...].T.astype(jnp.bfloat16)
-
     def all_sent(ref, sem):
         pltpu.make_async_copy(ref.at[all_but_one], ref.at[all_but_one], sem).wait()
 
@@ -431,11 +458,13 @@
         def _():
             halo_copy(n).wait_send()
 
-    all_sent(corr_send, c_send)
-    all_sent(corr_in, c_recv)
-
-
-def finish(values, corr_in, hit, f_out, a_out, image_out, image, out_sem):
+    all_sent(peak_send, c_send.at[0])
+    all_sent(corr_send, c_send.at[1])
+    all_sent(peak_in, c_recv.at[0])
+    all_sent(corr_in, c_recv.at[1])
+
+
+def finish(values, peak_in, corr_in, hit, f_out, a_out, image_out, image, out_sem):
     outs = [
         pltpu.make_async_copy(values.at[0], f_out.at[0], out_sem.at[0]),
         pltpu.make_async_copy(values.at[1], a_out.at[0], out_sem.at[1]),
@@ -443,9 +472,13 @@
     ]
     outs[0].start()
     outs[1].start()
-    tops = corr_in[:, 0].reshape(ROWS, CZ)
-    rests = corr_in[:, 1].reshape(ROWS, CZ)
-    image[...] = (mm(hit[...], tops) + mm(hit[...], rests)).reshape(SLAB, CY, CZ)
+    peak = peak_in[...]
+    peak = jnp.broadcast_to(jnp.concatenate([peak, peak], axis=2), (NS, 2 * CY, CZ))
+    share = corr_in[...].astype(jnp.int32).astype(jnp.float32) * (1.0 / STEPS)
+    rows = (share * peak).reshape(ROWS, CZ)
+    top = rows.astype(jnp.bfloat16)
+    rest = (rows - top.astype(jnp.float32)).astype(jnp.bfloat16)
+    image[...] = (mm(hit[...], top) + mm(hit[...], rest)).reshape(SLAB, CY, CZ)
     outs[2].start()
     for out in outs:
         out.wait()
@@ -469,6 +502,7 @@
         pltpu.VMEM((2, CX, CY, CZ), f32),
         pltpu.VMEM((2, ROWS, CZ), bf),
         pltpu.VMEM((2, ROWS, CZ), bf),
+        pltpu.VMEM((2, 4, CY, CZ), f32),
         pltpu.VMEM((2, XH, CZ), bf),
         pltpu.VMEM((SLAB, CY, CZ), bf),
         pltpu.VMEM((SLAB, CY, CZ), f32),
@@ -485,12 +519,14 @@
         pltpu.VMEM((NS, 2 * CY, CZ), bf),
         pltpu.VMEM((NS, 2 * CY, CZ), bf),
         pltpu.VMEM((2 * NS, CY, CZ), f32),
-        pltpu.VMEM((NS, 2, 2 * CY, CZ), bf),
+        pltpu.VMEM((NS, 1, CZ // 2), f32),
+        pltpu.VMEM((NS, 2 * CY, CZ), jnp.int16),
         pltpu.VMEM((ROWS, ROWS), f32),
         pltpu.SMEM((2, 1, 128), i32),
         pltpu.SMEM((1, 2), i32),
         pltpu.SMEM((1, 1), f32),
         dma((12,)),
+        dma((2,)),
         dma,
         dma,
         dma,
@@ -499,22 +535,23 @@
         dma((4,)),
         dma,
         dma((NS,)),
-        dma,
-        dma,
+        dma((2,)),
+        dma((2,)),
         pltpu.SemaphoreType.REGULAR((4,)),
         pltpu.SemaphoreType.REGULAR,
     ]
     anywhere = pl.BlockSpec(memory_space=pl.ANY)
     vmem = pl.BlockSpec(memory_space=pltpu.VMEM)
-    values, corr_in, hit = pl.pallas_call(
+    values, peak_in, corr_in, hit = pl.pallas_call(
         kernel,
         out_shape=(
             jax.ShapeDtypeStruct((2, CX, CY, CZ), f32),
-            jax.ShapeDtypeStruct((NS, 2, 2 * CY, CZ), bf),
+            jax.ShapeDtypeStruct((NS, 1, CZ // 2), f32),
+            jax.ShapeDtypeStruct((NS, 2 * CY, CZ), jnp.int16),
             jax.ShapeDtypeStruct((ROWS, ROWS), bf),
         ),
         in_specs=[anywhere] * 12,
-        out_specs=(vmem,) * 3,
+        out_specs=(vmem,) * 4,
         scratch_shapes=scratch,
         compiler_params=pltpu.CompilerParams(
             collective_id=0, has_side_effects=True, vmem_limit_bytes=LIMIT
@@ -523,11 +560,11 @@
     return pl.pallas_call(
         finish,
         out_shape=(field, field, field),
-        in_specs=[vmem] * 3,
+        in_specs=[vmem] * 4,
         out_specs=(anywhere,) * 3,
         scratch_shapes=[pltpu.VMEM((SLAB, CY, CZ), f32), dma((3,))],
         compiler_params=pltpu.CompilerParams(vmem_limit_bytes=LIMIT),
-    )(values, corr_in, hit)
+    )(values, peak_in, corr_in, hit)
 
 
 def solution(mesh):

time: 29.1 us -> 28.6 us (0.983)
  Pallas kernels: 27.7 us -> 27.1 us
    pallas_call x1, Pallas kernels: 26.7 us -> 26.1 us  [on_device(): pl.pallas_call(kernel, out_shape=(jax.ShapeDtypeStruct((2, CX, CY, CZ), f...]
where the time goes in v5:
time: 28.6 us; the launch traced here: 28.4 us
  Pallas kernels  27.1 us (95%)
  between operations  1.29 us (5%)
    pallas_call x1, Pallas kernels, on_device(): pl.pallas_call(kernel, out_shape=(jax.ShapeDtypeStruct((2, CX, CY, CZ), f...  26.1 us
    pallas_call x1, Pallas kernels, on_device(): pl.pallas_call(finish, out_shape=(field, field, field), in_specs=[vmem] *...  0.99 us

profile of v5, /device:TPU:1, one launch (start us, length us, event | category | flops | bytes accessed | tf_op | source)
XLA Modules:
  0.0 28.4 jit_solution(10014220730832966988)
XLA Ops:
  1.3 26.1 %shard_map.139 = (f32[2,32,8,256]{3,2,1,0:T(8,128)S(1)}, f32[16,1,128]{2,1,0:T(1,128)S(1)}, s16[16,16,256]{2,1,0:T(8,128)(2,1)S(1)}, bf16[256,256]{1,0:T(8,128)(2,1)S(1)}) custom-call(f32[1,32,8,256]{3,2,1,0:T(8,128)} %f_prev.1, f32[1,32,8,256]{3,2,1,0:T(8,128)} %f_now.1, f32[1,32,8,256]{3,2,1,0:T(8,128)} %a_prev.1, f32[1,32,8,256]{3,2,1,0:T(8,128)} %a_now.1, ...), custom_call_target="tpu_custom_call" | custom-call | tf_op jit(solution)/shard_map/pallas_call | solution.py:545
  27.4 1.0 %shard_map.140 = (f32[1,32,8,256]{3,2,1,0:T(8,128)}, f32[1,32,8,256]{3,2,1,0:T(8,128)}, f32[1,32,8,256]{3,2,1,0:T(8,128)}) custom-call(f32[2,32,8,256]{3,2,1,0:T(8,128)S(1)} %get-tuple-element.7.values, f32[16,1,128]{2,1,0:T(1,128)S(1)} %get-tuple-element.8.peak_in, s16[16,16,256]{2,1,0:T(8,128)(2,1)S(1)} %get-tuple-element.9.corr_in, ...), custom_call_target="tpu_custom_call" | custom-call | tf_op jit(solution)/shard_map/pallas_call | solution.py:560

commit v6 on v5

--- a/solution.py
+++ b/solution.py
@@ -23,6 +23,8 @@
 HALO = 2 * YH + 2 * XH
 STEPS = 32766.0
 TINY = 1e-34
+DIRECT = 3
+LATE = 6
 LIMIT = 40 * 1024 * 1024
 
 
@@ -69,11 +71,11 @@
     f_prev, f_now, a_prev, a_now, velocity, aperture, source_cell, strength, receivers, traces,
     square_hbm, halo_hbm,
     prev, peak_in, corr_in, hit_out,
-    now, lap, high, low, edge_f, edge, slab_b, slab, ids, cell_v, trace_v, square, halo_w,
+    now, lap, high, low, edge_f, edge, far, slab_b, slab, ids, cell_v, trace_v, square, halo_w,
     pick_send, halo, tables, wanted, wanted_by, blocks, arrived, speed, peak_send, corr_send,
     hit,
     smem_tables, source_s, strength_s,
-    load_sem, edge_sem, table_sem, id_sem, id_send, id_recv, halo_send, halo_recv, v_send, v_recv,
+    load_sem, edge_sem, far_send, far_recv, table_sem, id_sem, id_send, id_recv, halo_send, halo_recv, v_send, v_recv,
     c_send, c_recv, ready, go,
 ):
     me = lax.axis_index("shot")
@@ -99,7 +101,9 @@
         for field, now_hbm in enumerate((f_now, a_now))
     ]
 
-    @pl.when(lax.axis_index("tx") == 2)
+    direct = ty < DIRECT
+
+    @pl.when((tx == 2) & jnp.logical_not(direct))
     def _():
         edge_loads[0].start()
         edge_loads[1].start()
@@ -180,18 +184,35 @@
             ready.at[(1, 0, 3, 2)[n]], inc=1, device_id={axis: other}, device_id_type=MESH
         )
 
+    def far_copy(field):
+        return pltpu.make_async_remote_copy(
+            src_ref=(f_now, a_now)[field].at[0, 0:4],
+            dst_ref=far.at[field],
+            send_sem=far_send.at[field],
+            recv_sem=far_recv.at[field],
+            device_id={"tx": tx - 1},
+            device_id_type=MESH,
+        )
+
     def across():
         pl.semaphore_wait(barrier, 1)
         answer_first(3)
         halo_copy(3, edge).start()
 
-    @pl.when(relayed)
+    @pl.when(relayed & direct)
+    def _():
+        pl.semaphore_wait(barrier, 1)
+        answer_first(3)
+        far_copy(0).start()
+        far_copy(1).start()
+
+    @pl.when(relayed & jnp.logical_not(direct))
     def _():
         edge_loads[0].wait()
         edge_loads[1].wait()
         edge[...] = edge_f[...].reshape(2, XH, CZ).astype(jnp.bfloat16)
 
-    @pl.when(relayed & (ty < 6))
+    @pl.when(relayed & (ty >= DIRECT) & (ty < LATE))
     def _():
         across()
 
@@ -235,6 +256,10 @@
     def _():
         pl.semaphore_signal(go, inc=1, device_id={"tx": 2}, device_id_type=MESH)
 
+    @pl.when(relayed & (ty >= LATE))
+    def _():
+        across()
+
     @pl.when(relayed)
     def _():
         pl.semaphore_wait(go, 1)
@@ -250,10 +275,6 @@
         )
 
     each_partner(lambda d: id_copy(d).start())
-
-    @pl.when(relayed & (ty >= 6))
-    def _():
-        across()
 
     @pl.when(ty > 0)
     def _():
@@ -332,6 +353,8 @@
     loads[5].wait()
     loads[6].wait()
     loads[7].wait()
+    answer(0)
+
     all_but_one = pl.ds(0, NS - 1)
     pltpu.make_async_copy(wanted.at[all_but_one], wanted.at[all_but_one], id_recv).wait()
     id_local = pltpu.make_async_copy(wanted, wanted_by, id_sem)
@@ -345,8 +368,6 @@
         block_copy(d).start()
 
     arrived[me] = serve(me)
-    answer(0)
-
     @pl.when(ty >= 5)
     def _():
         answer(3)
@@ -385,17 +406,30 @@
         answer(2)
 
     halo_wait(2)
-    halo_wait(3)
+    near = halo[:, 2 * YH : 2 * YH + XH].astype(jnp.float32).reshape(2, 4, CY, CZ)
+
+    @pl.when((tx == 1) & direct)
+    def _():
+        far_copy(0).wait_recv()
+        far_copy(1).wait_recv()
+
+    @pl.when((tx < NTX - 1) & jnp.logical_not((tx == 1) & direct))
+    def _():
+        halo_copy(3).wait_recv()
+
+    @pl.when(jnp.logical_not((tx == 1) & direct))
+    def _():
+        far[...] = halo[:, 2 * YH + XH :].astype(jnp.float32).reshape(2, 4, CY, CZ)
+
     for field in range(2):
-        layers = halo[field, 2 * YH :].astype(jnp.float32).reshape(8, CY, CZ)
         for q in range(4):
             for x in range(4):
                 if x <= q:
                     weight = STENCIL_WEIGHTS[x + 4 - q]
-                    lap[field, x] = lap[field, x] + weight * layers[q]
+                    lap[field, x] = lap[field, x] + weight * near[field, q]
                 if x >= q:
                     weight = STENCIL_WEIGHTS[4 + q - x]
-                    lap[field, CX - 4 + x] = lap[field, CX - 4 + x] + weight * layers[4 + q]
+                    lap[field, CX - 4 + x] = lap[field, CX - 4 + x] + weight * far[field, q]
 
     table_copy.wait()
 
@@ -452,11 +486,20 @@
 
     all_sent(wanted, id_send)
     all_sent(blocks, v_send)
-    for n in range(4):
+    for n in range(3):
 
         @pl.when(sides[n][0])
         def _():
             halo_copy(n).wait_send()
+
+    @pl.when((tx > 0) & jnp.logical_not(relayed & direct))
+    def _():
+        halo_copy(3).wait_send()
+
+    @pl.when(relayed & direct)
+    def _():
+        far_copy(0).wait_send()
+        far_copy(1).wait_send()
 
     all_sent(peak_send, c_send.at[0])
     all_sent(corr_send, c_send.at[1])
@@ -504,6 +547,7 @@
         pltpu.VMEM((2, ROWS, CZ), bf),
         pltpu.VMEM((2, 4, CY, CZ), f32),
         pltpu.VMEM((2, XH, CZ), bf),
+        pltpu.VMEM((2, 4, CY, CZ), f32),
         pltpu.VMEM((SLAB, CY, CZ), bf),
         pltpu.VMEM((SLAB, CY, CZ), f32),
         pltpu.VMEM((1, CX), i32),
@@ -526,6 +570,8 @@
         pltpu.SMEM((1, 2), i32),
         pltpu.SMEM((1, 1), f32),
         dma((12,)),
+        dma((2,)),
+        dma((2,)),
         dma((2,)),
         dma,
         dma,

time: 28.6 us -> 28.5 us (level)
  no operation moved by 1% of the time
where the time goes in v6:
time: 28.5 us; the launch traced here: 28.3 us
  Pallas kernels  27 us (95%)
  between operations  1.29 us (5%)
    pallas_call x1, Pallas kernels, on_device(): pl.pallas_call(kernel, out_shape=(jax.ShapeDtypeStruct((2, CX, CY, CZ), f...  26 us
    pallas_call x1, Pallas kernels, on_device(): pl.pallas_call(finish, out_shape=(field, field, field), in_specs=[vmem] *...  0.99 us

profile of v6, /device:TPU:1, one launch (start us, length us, event | category | flops | bytes accessed | tf_op | source)
XLA Modules:
  0.0 28.3 jit_solution(2768683969052783305)
XLA Ops:
  1.3 26.0 %shard_map.139 = (f32[2,32,8,256]{3,2,1,0:T(8,128)S(1)}, f32[16,1,128]{2,1,0:T(1,128)S(1)}, s16[16,16,256]{2,1,0:T(8,128)(2,1)S(1)}, bf16[256,256]{1,0:T(8,128)(2,1)S(1)}) custom-call(f32[1,32,8,256]{3,2,1,0:T(8,128)} %f_prev.1, f32[1,32,8,256]{3,2,1,0:T(8,128)} %f_now.1, f32[1,32,8,256]{3,2,1,0:T(8,128)} %a_prev.1, f32[1,32,8,256]{3,2,1,0:T(8,128)} %a_now.1, ...), custom_call_target="tpu_custom_call" | custom-call | tf_op jit(solution)/shard_map/pallas_call | solution.py:591
  27.3 1.0 %shard_map.140 = (f32[1,32,8,256]{3,2,1,0:T(8,128)}, f32[1,32,8,256]{3,2,1,0:T(8,128)}, f32[1,32,8,256]{3,2,1,0:T(8,128)}) custom-call(f32[2,32,8,256]{3,2,1,0:T(8,128)S(1)} %get-tuple-element.7.values, f32[16,1,128]{2,1,0:T(1,128)S(1)} %get-tuple-element.8.peak_in, s16[16,16,256]{2,1,0:T(8,128)(2,1)S(1)} %get-tuple-element.9.corr_in, ...), custom_call_target="tpu_custom_call" | custom-call | tf_op jit(solution)/shard_map/pallas_call | solution.py:606

commit v7 on v6

--- a/solution.py
+++ b/solution.py
@@ -57,10 +57,21 @@
     return square, np.concatenate(parts(halo), axis=0)
 
 
-def each_partner(body):
-    @pl.loop(1, NS)
+def each_partner(body, near=0):
+    me = lax.axis_index("shot")
+    x, y = me // 4, lax.rem(me, 4)
+    turn_x, turn_y = (x < 2).astype(jnp.int32), (y < 2).astype(jnp.int32)
+
+    @pl.loop(0, NS)
     def _(step):
-        body(lax.rem(5 * step, NS))
+        step = step + near * (NS - 1 - 2 * step)
+        i, j = step // 4, lax.rem(step, 4)
+        other = 4 * (i + turn_x * (3 - 2 * i)) + j + turn_y * (3 - 2 * j)
+        d = lax.rem(other - me + NS, NS)
+
+        @pl.when(d > 0)
+        def _():
+            body(d)
 
 
 def mm(a, b):
@@ -256,7 +267,9 @@
     def _():
         pl.semaphore_signal(go, inc=1, device_id={"tx": 2}, device_id_type=MESH)
 
-    @pl.when(relayed & (ty >= LATE))
+    upper = me // 4 + lax.rem(me, 4) >= 2
+
+    @pl.when(relayed & (ty >= LATE) & jnp.logical_not(upper))
     def _():
         across()
 
@@ -275,6 +288,10 @@
         )
 
     each_partner(lambda d: id_copy(d).start())
+
+    @pl.when(relayed & (ty >= LATE) & upper)
+    def _():
+        across()
 
     @pl.when(ty > 0)
     def _():
@@ -362,10 +379,10 @@
     id_local.wait()
 
     @each_partner
-    def _(d):
-        shot = lax.rem(me - d + NS, NS)
+    def _(ahead):
+        shot = lax.rem(me + ahead, NS)
         blocks[shot] = serve(shot)
-        block_copy(d).start()
+        block_copy(NS - ahead).start()
 
     arrived[me] = serve(me)
     @pl.when(ty >= 5)
@@ -467,13 +484,14 @@
 
     peak_in[me], corr_in[me] = contribute(me)
 
-    @each_partner
-    def _(d):
+    def one_owner(d):
         block_copy(d).wait_recv()
         owner = lax.rem(me + d, NS)
         peak_send[owner], corr_send[owner] = contribute(owner)
         for copy in corr_copies(d):
             copy.start()
+
+    each_partner(one_owner, near=((tx == 0) | (tx == 3)).astype(jnp.int32))
 
     @pl.loop(0, CX)
     def _(r):

time: 28.5 us -> 28.4 us (level)
  no operation moved by 1% of the time
where the time goes in v7:
time: 28.4 us; the launch traced here: 28.2 us
  Pallas kernels  26.9 us (95%)
  between operations  1.29 us (5%)
    pallas_call x1, Pallas kernels, on_device(): pl.pallas_call(kernel, out_shape=(jax.ShapeDtypeStruct((2, CX, CY, CZ), f...  25.9 us
    pallas_call x1, Pallas kernels, on_device(): pl.pallas_call(finish, out_shape=(field, field, field), in_specs=[vmem] *...  0.99 us

profile of v7, /device:TPU:1, one launch (start us, length us, event | category | flops | bytes accessed | tf_op | source)
XLA Modules:
  0.0 28.2 jit_solution(436462500765891548)
XLA Ops:
  1.3 25.9 %shard_map.139 = (f32[2,32,8,256]{3,2,1,0:T(8,128)S(1)}, f32[16,1,128]{2,1,0:T(1,128)S(1)}, s16[16,16,256]{2,1,0:T(8,128)(2,1)S(1)}, bf16[256,256]{1,0:T(8,128)(2,1)S(1)}) custom-call(f32[1,32,8,256]{3,2,1,0:T(8,128)} %f_prev.1, f32[1,32,8,256]{3,2,1,0:T(8,128)} %f_now.1, f32[1,32,8,256]{3,2,1,0:T(8,128)} %a_prev.1, f32[1,32,8,256]{3,2,1,0:T(8,128)} %a_now.1, ...), custom_call_target="tpu_custom_call" | custom-call | tf_op jit(solution)/shard_map/pallas_call | solution.py:609
  27.2 1.0 %shard_map.140 = (f32[1,32,8,256]{3,2,1,0:T(8,128)}, f32[1,32,8,256]{3,2,1,0:T(8,128)}, f32[1,32,8,256]{3,2,1,0:T(8,128)}) custom-call(f32[2,32,8,256]{3,2,1,0:T(8,128)S(1)} %get-tuple-element.7.values, f32[16,1,128]{2,1,0:T(1,128)S(1)} %get-tuple-element.8.peak_in, s16[16,16,256]{2,1,0:T(8,128)(2,1)S(1)} %get-tuple-element.9.corr_in, ...), custom_call_target="tpu_custom_call" | custom-call | tf_op jit(solution)/shard_map/pallas_call | solution.py:624

commit v8 on v6

--- a/solution.py
+++ b/solution.py
@@ -23,7 +23,7 @@
 HALO = 2 * YH + 2 * XH
 STEPS = 32766.0
 TINY = 1e-34
-DIRECT = 3
+DIRECT = 1
 LATE = 6
 LIMIT = 40 * 1024 * 1024
 
@@ -57,10 +57,22 @@
     return square, np.concatenate(parts(halo), axis=0)
 
 
-def each_partner(body):
-    @pl.loop(1, NS)
-    def _(step):
-        body(lax.rem(5 * step, NS))
+def each_partner(body, near=0):
+    me = lax.axis_index("shot")
+    turn_x = (me < NS // 2).astype(jnp.int32)
+    turn_y = (lax.rem(me, 4) < 2).astype(jnp.int32)
+    turn_x = turn_x + near * (1 - 2 * turn_x)
+    turn_y = turn_y + near * (1 - 2 * turn_y)
+    corner, step_x, step_y = 12 * turn_x + 3 * turn_y, 4 - 8 * turn_x, 1 - 2 * turn_y
+
+    @pl.loop(0, 4)
+    def _(i):
+        for j in range(4):
+            other = corner + step_x * i + step_y * j
+
+            @pl.when(other != me)
+            def _():
+                body(other)
 
 
 def mm(a, b):
@@ -139,9 +151,10 @@
             barrier, inc=1, device_id={"tx": home, "ty": ty + 1}, device_id_type=MESH
         )
 
-    for n in (2, 3):
-
-        @pl.when(first[n])
+    mutual = ty >= LATE
+    for n, says in ((2, first[2]), (3, first[3] | (relayed & mutual))):
+
+        @pl.when(says)
         def _():
             pl.semaphore_signal(
                 barrier, inc=1, device_id={"tx": sides[n][2]}, device_id_type=MESH
@@ -196,7 +209,11 @@
 
     def across():
         pl.semaphore_wait(barrier, 1)
-        answer_first(3)
+
+        @pl.when(jnp.logical_not(mutual))
+        def _():
+            answer_first(3)
+
         halo_copy(3, edge).start()
 
     @pl.when(relayed & direct)
@@ -212,7 +229,7 @@
         edge_loads[1].wait()
         edge[...] = edge_f[...].reshape(2, XH, CZ).astype(jnp.bfloat16)
 
-    @pl.when(relayed & (ty >= DIRECT) & (ty < LATE))
+    @pl.when(relayed & (ty >= DIRECT) & jnp.logical_not(mutual))
     def _():
         across()
 
@@ -246,6 +263,7 @@
         pick_send[1, field] = picked[YH:]
 
     partners = NS - 1 + (ty > 0).astype(jnp.int32) + (tx == 0).astype(jnp.int32)
+    partners = partners + ((tx == 1) & mutual).astype(jnp.int32)
     partners = partners + jnp.where(tx == 3, NS + (ty > 0).astype(jnp.int32), 0)
 
     @pl.when(jnp.logical_not(relayed))
@@ -256,7 +274,9 @@
     def _():
         pl.semaphore_signal(go, inc=1, device_id={"tx": 2}, device_id_type=MESH)
 
-    @pl.when(relayed & (ty >= LATE))
+    upper = me // 4 + lax.rem(me, 4) >= 2
+
+    @pl.when(relayed & mutual & jnp.logical_not(upper))
     def _():
         across()
 
@@ -264,17 +284,21 @@
     def _():
         pl.semaphore_wait(go, 1)
 
-    def id_copy(d):
+    def id_copy(other):
         return pltpu.make_async_remote_copy(
             src_ref=wanted.at[me],
             dst_ref=wanted.at[me],
             send_sem=id_send,
             recv_sem=id_recv,
-            device_id={"shot": lax.rem(me + d, NS)},
+            device_id={"shot": other},
             device_id_type=MESH,
         )
 
-    each_partner(lambda d: id_copy(d).start())
+    each_partner(lambda other: id_copy(other).start())
+
+    @pl.when(relayed & mutual & upper)
+    def _():
+        across()
 
     @pl.when(ty > 0)
     def _():
@@ -284,7 +308,7 @@
     def _():
         answer_first(2)
 
-    @pl.when(jnp.logical_not(odd))
+    @pl.when(jnp.logical_not(odd) | ((tx == 1) & mutual))
     def _():
         halo_copy(2).start()
 
@@ -309,13 +333,12 @@
         rows = [slab[wanted_by[shot, 0, 2 * me + k]] for k in range(2)]
         return jnp.concatenate(rows, axis=0).astype(jnp.bfloat16)
 
-    def block_copy(d):
-        shot = lax.rem(me - d + NS, NS)
+    def block_copy(owner, shot):
         return pltpu.make_async_remote_copy(
             src_ref=blocks.at[shot],
-            dst_ref=arrived.at[me],
+            dst_ref=arrived.at[owner],
             send_sem=v_send,
-            recv_sem=v_recv.at[d],
+            recv_sem=v_recv.at[owner],
             device_id={"shot": shot},
             device_id_type=MESH,
         )
@@ -362,16 +385,18 @@
     id_local.wait()
 
     @each_partner
-    def _(d):
-        shot = lax.rem(me - d + NS, NS)
+    def _(shot):
         blocks[shot] = serve(shot)
-        block_copy(d).start()
+        block_copy(me, shot).start()
 
     arrived[me] = serve(me)
     @pl.when(ty >= 5)
     def _():
         answer(3)
-        answer(2)
+
+        @pl.when(jnp.logical_not(mutual))
+        def _():
+            answer(2)
 
     depth_l = lax.broadcasted_iota(jnp.int32, (CY, ROWS), 1)
     same_y = (depth_l & (CY - 1)) == lax.broadcasted_iota(jnp.int32, (CY, ROWS), 0)
@@ -433,8 +458,7 @@
 
     table_copy.wait()
 
-    def corr_copies(d):
-        owner = lax.rem(me + d, NS)
+    def corr_copies(owner):
         return [
             pltpu.make_async_remote_copy(
                 src_ref=source.at[owner],
@@ -467,13 +491,13 @@
 
     peak_in[me], corr_in[me] = contribute(me)
 
-    @each_partner
-    def _(d):
-        block_copy(d).wait_recv()
-        owner = lax.rem(me + d, NS)
+    def one_owner(owner):
+        block_copy(owner, me).wait_recv()
         peak_send[owner], corr_send[owner] = contribute(owner)
-        for copy in corr_copies(d):
+        for copy in corr_copies(owner):
             copy.start()
+
+    each_partner(one_owner, near=((tx == 0) | (tx == 3)).astype(jnp.int32))
 
     @pl.loop(0, CX)
     def _(r):

time: 28.5 us -> 27.9 us (0.979)
  Pallas kernels: 27 us -> 26.4 us
    pallas_call x1, Pallas kernels: 26 us -> 25.4 us  [on_device(): pl.pallas_call(kernel, out_shape=(jax.ShapeDtypeStruct((2, CX, CY, CZ), f...]
where the time goes in v8:
time: 27.9 us; the launch traced here: 27.7 us
  Pallas kernels  26.4 us (95%)
  between operations  1.29 us (5%)
    pallas_call x1, Pallas kernels, on_device(): pl.pallas_call(kernel, out_shape=(jax.ShapeDtypeStruct((2, CX, CY, CZ), f...  25.4 us
    pallas_call x1, Pallas kernels, on_device(): pl.pallas_call(finish, out_shape=(field, field, field), in_specs=[vmem] *...  0.99 us

profile of v8, /device:TPU:1, one launch (start us, length us, event | category | flops | bytes accessed | tf_op | source)
XLA Modules:
  0.0 27.7 jit_solution(5935686436272701543)
XLA Ops:
  1.3 25.4 %shard_map.139 = (f32[2,32,8,256]{3,2,1,0:T(8,128)S(1)}, f32[16,1,128]{2,1,0:T(1,128)S(1)}, s16[16,16,256]{2,1,0:T(8,128)(2,1)S(1)}, bf16[256,256]{1,0:T(8,128)(2,1)S(1)}) custom-call(f32[1,32,8,256]{3,2,1,0:T(8,128)} %f_prev.1, f32[1,32,8,256]{3,2,1,0:T(8,128)} %f_now.1, f32[1,32,8,256]{3,2,1,0:T(8,128)} %a_prev.1, f32[1,32,8,256]{3,2,1,0:T(8,128)} %a_now.1, ...), custom_call_target="tpu_custom_call" | custom-call | tf_op jit(solution)/shard_map/pallas_call | solution.py:615
  26.7 1.0 %shard_map.140 = (f32[1,32,8,256]{3,2,1,0:T(8,128)}, f32[1,32,8,256]{3,2,1,0:T(8,128)}, f32[1,32,8,256]{3,2,1,0:T(8,128)}) custom-call(f32[2,32,8,256]{3,2,1,0:T(8,128)S(1)} %get-tuple-element.7.values, f32[16,1,128]{2,1,0:T(1,128)S(1)} %get-tuple-element.8.peak_in, s16[16,16,256]{2,1,0:T(8,128)(2,1)S(1)} %get-tuple-element.9.corr_in, ...), custom_call_target="tpu_custom_call" | custom-call | tf_op jit(solution)/shard_map/pallas_call | solution.py:630

commit v9 on v8

--- a/solution.py
+++ b/solution.py
@@ -67,7 +67,8 @@
 
     @pl.loop(0, 4)
     def _(i):
-        for j in range(4):
+        @pl.loop(0, 4)
+        def _(j):
             other = corner + step_x * i + step_y * j
 
             @pl.when(other != me)
@@ -136,6 +137,38 @@
 
     barrier = pltpu.get_barrier_semaphore()
 
+    mutual = ty >= LATE
+    for n, says in ((2, first[2]), (3, first[3] | (relayed & mutual))):
+
+        @pl.when(says)
+        def _():
+            pl.semaphore_signal(
+                barrier, inc=1, device_id={"tx": sides[n][2]}, device_id_type=MESH
+            )
+
+    def answer_first(n):
+        axis, other = sides[n][1:]
+        pl.semaphore_signal(
+            ready.at[(1, 0, 3, 2)[n]], inc=1, device_id={axis: other}, device_id_type=MESH
+        )
+
+    def far_copy(field):
+        return pltpu.make_async_remote_copy(
+            src_ref=(f_now, a_now)[field].at[0, 0:4],
+            dst_ref=far.at[field],
+            send_sem=far_send.at[field],
+            recv_sem=far_recv.at[field],
+            device_id={"tx": tx - 1},
+            device_id_type=MESH,
+        )
+
+    @pl.when(relayed & direct)
+    def _():
+        pl.semaphore_wait(barrier, 1)
+        far_copy(0).start()
+        far_copy(1).start()
+        answer_first(3)
+
     @pl.loop(1 - relayed.astype(jnp.int32), NS)
     def _(d):
         pl.semaphore_signal(
@@ -150,15 +183,6 @@
         pl.semaphore_signal(
             barrier, inc=1, device_id={"tx": home, "ty": ty + 1}, device_id_type=MESH
         )
-
-    mutual = ty >= LATE
-    for n, says in ((2, first[2]), (3, first[3] | (relayed & mutual))):
-
-        @pl.when(says)
-        def _():
-            pl.semaphore_signal(
-                barrier, inc=1, device_id={"tx": sides[n][2]}, device_id_type=MESH
-            )
 
     for n in (3, 5, 6, 7, 8, 9, 10, 11):
         loads[n].start()
@@ -191,22 +215,6 @@
             device_id_type=MESH,
         )
 
-    def answer_first(n):
-        axis, other = sides[n][1:]
-        pl.semaphore_signal(
-            ready.at[(1, 0, 3, 2)[n]], inc=1, device_id={axis: other}, device_id_type=MESH
-        )
-
-    def far_copy(field):
-        return pltpu.make_async_remote_copy(
-            src_ref=(f_now, a_now)[field].at[0, 0:4],
-            dst_ref=far.at[field],
-            send_sem=far_send.at[field],
-            recv_sem=far_recv.at[field],
-            device_id={"tx": tx - 1},
-            device_id_type=MESH,
-        )
-
     def across():
         pl.semaphore_wait(barrier, 1)
 
@@ -216,13 +224,6 @@
 
         halo_copy(3, edge).start()
 
-    @pl.when(relayed & direct)
-    def _():
-        pl.semaphore_wait(barrier, 1)
-        answer_first(3)
-        far_copy(0).start()
-        far_copy(1).start()
-
     @pl.when(relayed & jnp.logical_not(direct))
     def _():
         edge_loads[0].wait()
@@ -235,7 +236,9 @@
 
     loads[1].wait()
     loads[2].wait()
-    for field in range(2):
+
+    @pl.loop(0, 2)
+    def _(field):
         u = now[field].reshape(ROWS, CZ)
         top = u.astype(jnp.bfloat16)
         high[field] = top
@@ -257,7 +260,9 @@
     table_copy.start()
 
     loads[3].wait()
-    for field in range(2):
+
+    @pl.loop(0, 2)
+    def _(field):
         picked = mm(square[4 * ROWS : 5 * ROWS, :], high[field]).astype(jnp.bfloat16)
         pick_send[0, field] = picked[0:YH]
         pick_send[1, field] = picked[YH:]
@@ -343,7 +348,8 @@
             device_id_type=MESH,
         )
 
-    for field in range(2):
+    @pl.loop(0, 2)
+    def _(field):
         top, rest = high[field], low[field]
         lap[field] = (
             mm(square[0:ROWS, :], top)
@@ -418,7 +424,9 @@
 
     halo_wait(0)
     halo_wait(1)
-    for field, extra in ((0, injected), (1, recorded)):
+    @pl.loop(0, 2)
+    def _(field):
+        extra = jnp.where(field == 0, injected, recorded)
         layers = halo[field, 0 : 2 * YH]
         beyond = mm(halo_w[0:ROWS, :], layers) + mm(halo_w[ROWS:, :], layers)
         beyond = beyond + jnp.where(surface, jnp.broadcast_to(extra, (ROWS, CZ)), 0.0)
@@ -431,7 +439,6 @@
         answer(2)
 
     halo_wait(2)
-    near = halo[:, 2 * YH : 2 * YH + XH].astype(jnp.float32).reshape(2, 4, CY, CZ)
 
     @pl.when((tx == 1) & direct)
     def _():
@@ -446,12 +453,14 @@
     def _():
         far[...] = halo[:, 2 * YH + XH :].astype(jnp.float32).reshape(2, 4, CY, CZ)
 
-    for field in range(2):
+    @pl.loop(0, 2)
+    def _(field):
+        near = halo[field, 2 * YH : 2 * YH + XH].astype(jnp.float32).reshape(4, CY, CZ)
         for q in range(4):
             for x in range(4):
                 if x <= q:
                     weight = STENCIL_WEIGHTS[x + 4 - q]
-                    lap[field, x] = lap[field, x] + weight * near[field, q]
+                    lap[field, x] = lap[field, x] + weight * near[q]
                 if x >= q:
                     weight = STENCIL_WEIGHTS[4 + q - x]
                     lap[field, CX - 4 + x] = lap[field, CX - 4 + x] + weight * far[field, q]

time: 27.9 us -> 28.2 us (1.011)
  Pallas kernels: 26.4 us -> 26.7 us
    pallas_call x1, Pallas kernels: 25.4 us -> 25.7 us  [on_device(): pl.pallas_call(kernel, out_shape=(jax.ShapeDtypeStruct((2, CX, CY, CZ), f...]
where the time goes in v9:
time: 28.2 us; the launch traced here: 28 us
  Pallas kernels  26.7 us (95%)
  between operations  1.29 us (5%)
    pallas_call x1, Pallas kernels, on_device(): pl.pallas_call(kernel, out_shape=(jax.ShapeDtypeStruct((2, CX, CY, CZ), f...  25.7 us
    pallas_call x1, Pallas kernels, on_device(): pl.pallas_call(finish, out_shape=(field, field, field), in_specs=[vmem] *...  0.99 us

profile of v9, /device:TPU:1, one launch (start us, length us, event | category | flops | bytes accessed | tf_op | source)
XLA Modules:
  0.0 28.0 jit_solution(6629727400009908409)
XLA Ops:
  1.3 25.7 %shard_map.139 = (f32[2,32,8,256]{3,2,1,0:T(8,128)S(1)}, f32[16,1,128]{2,1,0:T(1,128)S(1)}, s16[16,16,256]{2,1,0:T(8,128)(2,1)S(1)}, bf16[256,256]{1,0:T(8,128)(2,1)S(1)}) custom-call(f32[1,32,8,256]{3,2,1,0:T(8,128)} %f_prev.1, f32[1,32,8,256]{3,2,1,0:T(8,128)} %f_now.1, f32[1,32,8,256]{3,2,1,0:T(8,128)} %a_prev.1, f32[1,32,8,256]{3,2,1,0:T(8,128)} %a_now.1, ...), custom_call_target="tpu_custom_call" | custom-call | tf_op jit(solution)/shard_map/pallas_call | solution.py:624
  27.0 1.0 %shard_map.140 = (f32[1,32,8,256]{3,2,1,0:T(8,128)}, f32[1,32,8,256]{3,2,1,0:T(8,128)}, f32[1,32,8,256]{3,2,1,0:T(8,128)}) custom-call(f32[2,32,8,256]{3,2,1,0:T(8,128)S(1)} %get-tuple-element.7.values, f32[16,1,128]{2,1,0:T(1,128)S(1)} %get-tuple-element.8.peak_in, s16[16,16,256]{2,1,0:T(8,128)(2,1)S(1)} %get-tuple-element.9.corr_in, ...), custom_call_target="tpu_custom_call" | custom-call | tf_op jit(solution)/shard_map/pallas_call | solution.py:639

commit v10 on v9

--- a/solution.py
+++ b/solution.py
@@ -57,7 +57,7 @@
     return square, np.concatenate(parts(halo), axis=0)
 
 
-def each_partner(body, near=0):
+def each_partner(body, near=0, row=None):
     me = lax.axis_index("shot")
     turn_x = (me < NS // 2).astype(jnp.int32)
     turn_y = (lax.rem(me, 4) < 2).astype(jnp.int32)
@@ -67,6 +67,9 @@
 
     @pl.loop(0, 4)
     def _(i):
+        if row is not None:
+            row(3 * turn_x + (1 - 2 * turn_x) * i)
+
         @pl.loop(0, 4)
         def _(j):
             other = corner + step_x * i + step_y * j
@@ -88,7 +91,7 @@
     pick_send, halo, tables, wanted, wanted_by, blocks, arrived, speed, peak_send, corr_send,
     hit,
     smem_tables, source_s, strength_s,
-    load_sem, edge_sem, far_send, far_recv, table_sem, id_sem, id_send, id_recv, halo_send, halo_recv, v_send, v_recv,
+    load_sem, edge_sem, far_sem, table_sem, id_sem, id_send, id_recv, halo_send, halo_recv, v_send, v_recv,
     c_send, c_recv, ready, go,
 ):
     me = lax.axis_index("shot")
@@ -98,19 +101,19 @@
     loads = [
         pltpu.make_async_copy(aperture.at[0], ids, load_sem.at[0]),
         pltpu.make_async_copy(f_now.at[0], now.at[0], load_sem.at[1]),
-        pltpu.make_async_copy(a_now.at[0], now.at[1], load_sem.at[2]),
+        pltpu.make_async_copy(a_now.at[0], now.at[1], load_sem.at[1]),
         pltpu.make_async_copy(square_hbm, square, load_sem.at[3]),
         pltpu.make_async_copy(velocity.at[0], slab_b, load_sem.at[4]),
         pltpu.make_async_copy(halo_hbm, halo_w, load_sem.at[5]),
         pltpu.make_async_copy(f_prev.at[0], prev.at[0], load_sem.at[6]),
-        pltpu.make_async_copy(a_prev.at[0], prev.at[1], load_sem.at[7]),
+        pltpu.make_async_copy(a_prev.at[0], prev.at[1], load_sem.at[6]),
         pltpu.make_async_copy(receivers.at[0], cell_v, load_sem.at[8]),
         pltpu.make_async_copy(traces, trace_v, load_sem.at[9]),
-        pltpu.make_async_copy(source_cell, source_s, load_sem.at[10]),
-        pltpu.make_async_copy(strength, strength_s, load_sem.at[11]),
+        pltpu.make_async_copy(source_cell, source_s, load_sem.at[2]),
+        pltpu.make_async_copy(strength, strength_s, load_sem.at[7]),
     ]
     edge_loads = [
-        pltpu.make_async_copy(now_hbm.at[0, 0:4], edge_f.at[field], edge_sem.at[field])
+        pltpu.make_async_copy(now_hbm.at[0, 0:4], edge_f.at[field], edge_sem)
         for field, now_hbm in enumerate((f_now, a_now))
     ]
 
@@ -152,12 +155,12 @@
             ready.at[(1, 0, 3, 2)[n]], inc=1, device_id={axis: other}, device_id_type=MESH
         )
 
-    def far_copy(field):
+    def far_copy(field, x):
         return pltpu.make_async_remote_copy(
-            src_ref=(f_now, a_now)[field].at[0, 0:4],
-            dst_ref=far.at[field],
-            send_sem=far_send.at[field],
-            recv_sem=far_recv.at[field],
+            src_ref=(f_now, a_now)[field].at[0, x],
+            dst_ref=far.at[field, x],
+            send_sem=far_sem.at[0],
+            recv_sem=far_sem.at[1],
             device_id={"tx": tx - 1},
             device_id_type=MESH,
         )
@@ -165,8 +168,9 @@
     @pl.when(relayed & direct)
     def _():
         pl.semaphore_wait(barrier, 1)
-        far_copy(0).start()
-        far_copy(1).start()
+        for x in range(4):
+            far_copy(0, x).start()
+            far_copy(1, x).start()
         answer_first(3)
 
     @pl.loop(1 - relayed.astype(jnp.int32), NS)
@@ -226,16 +230,14 @@
 
     @pl.when(relayed & jnp.logical_not(direct))
     def _():
-        edge_loads[0].wait()
-        edge_loads[1].wait()
+        pltpu.make_async_copy(edge_f, edge_f, edge_sem).wait()
         edge[...] = edge_f[...].reshape(2, XH, CZ).astype(jnp.bfloat16)
 
     @pl.when(relayed & (ty >= DIRECT) & jnp.logical_not(mutual))
     def _():
         across()
 
-    loads[1].wait()
-    loads[2].wait()
+    pltpu.make_async_copy(now, now, load_sem.at[1]).wait()
 
     @pl.loop(0, 2)
     def _(field):
@@ -343,7 +345,7 @@
             src_ref=blocks.at[shot],
             dst_ref=arrived.at[owner],
             send_sem=v_send,
-            recv_sem=v_recv.at[owner],
+            recv_sem=v_recv.at[me // 4],
             device_id={"shot": shot},
             device_id_type=MESH,
         )
@@ -380,8 +382,7 @@
     surface = lax.broadcasted_iota(jnp.int32, (ROWS, CZ), 1) == SURFACE_DEPTH
 
     loads[5].wait()
-    loads[6].wait()
-    loads[7].wait()
+    pltpu.make_async_copy(prev, prev, load_sem.at[6]).wait()
     answer(0)
 
     all_but_one = pl.ds(0, NS - 1)
@@ -442,8 +443,7 @@
 
     @pl.when((tx == 1) & direct)
     def _():
-        far_copy(0).wait_recv()
-        far_copy(1).wait_recv()
+        pltpu.make_async_copy(far, far, far_sem.at[1]).wait()
 
     @pl.when((tx < NTX - 1) & jnp.logical_not((tx == 1) & direct))
     def _():
@@ -501,12 +501,19 @@
     peak_in[me], corr_in[me] = contribute(me)
 
     def one_owner(owner):
-        block_copy(owner, me).wait_recv()
         peak_send[owner], corr_send[owner] = contribute(owner)
         for copy in corr_copies(owner):
             copy.start()
 
-    each_partner(one_owner, near=((tx == 0) | (tx == 3)).astype(jnp.int32))
+    def row_of_blocks(x):
+        for mine, count in ((x == me // 4, 3), (x != me // 4, 4)):
+
+            @pl.when(mine)
+            def _():
+                four = arrived.at[pl.ds(4 * x, count)]
+                pltpu.make_async_copy(four, four, v_recv.at[x]).wait()
+
+    each_partner(one_owner, ((tx == 0) | (tx == 3)).astype(jnp.int32), row_of_blocks)
 
     @pl.loop(0, CX)
     def _(r):
@@ -531,8 +538,7 @@
 
     @pl.when(relayed & direct)
     def _():
-        far_copy(0).wait_send()
-        far_copy(1).wait_send()
+        pltpu.make_async_copy(far, far, far_sem.at[0]).wait()
 
     all_sent(peak_send, c_send.at[0])
     all_sent(corr_send, c_send.at[1])
@@ -602,9 +608,8 @@
         pltpu.SMEM((2, 1, 128), i32),
         pltpu.SMEM((1, 2), i32),
         pltpu.SMEM((1, 1), f32),
-        dma((12,)),
-        dma((2,)),
-        dma((2,)),
+        dma((10,)),
+        dma,
         dma((2,)),
         dma,
         dma,
@@ -613,7 +618,7 @@
         dma((4,)),
         dma((4,)),
         dma,
-        dma((NS,)),
+        dma((4,)),
         dma((2,)),
         dma((2,)),
         pltpu.SemaphoreType.REGULAR((4,)),

time: 28.2 us -> 27.6 us (0.979)
  Pallas kernels: 26.7 us -> 26.2 us
    pallas_call x1, Pallas kernels: 25.7 us -> 25.2 us  [on_device(): pl.pallas_call(kernel, out_shape=(jax.ShapeDtypeStruct((2, CX, CY, CZ), f...]
where the time goes in v10:
time: 27.6 us; the launch traced here: 27.5 us
  Pallas kernels  26.2 us (95%)
  between operations  1.29 us (5%)
    pallas_call x1, Pallas kernels, on_device(): pl.pallas_call(kernel, out_shape=(jax.ShapeDtypeStruct((2, CX, CY, CZ), f...  25.2 us
    pallas_call x1, Pallas kernels, on_device(): pl.pallas_call(finish, out_shape=(field, field, field), in_specs=[vmem] *...  0.99 us

profile of v10, /device:TPU:1, one launch (start us, length us, event | category | flops | bytes accessed | tf_op | source)
XLA Modules:
  0.0 27.5 jit_solution(17040685260425079925)
XLA Ops:
  1.3 25.2 %shard_map.139 = (f32[2,32,8,256]{3,2,1,0:T(8,128)S(1)}, f32[16,1,128]{2,1,0:T(1,128)S(1)}, s16[16,16,256]{2,1,0:T(8,128)(2,1)S(1)}, bf16[256,256]{1,0:T(8,128)(2,1)S(1)}) custom-call(f32[1,32,8,256]{3,2,1,0:T(8,128)} %f_prev.1, f32[1,32,8,256]{3,2,1,0:T(8,128)} %f_now.1, f32[1,32,8,256]{3,2,1,0:T(8,128)} %a_prev.1, f32[1,32,8,256]{3,2,1,0:T(8,128)} %a_now.1, ...), custom_call_target="tpu_custom_call" | custom-call | tf_op jit(solution)/shard_map/pallas_call | solution.py:629
  26.5 1.0 %shard_map.140 = (f32[1,32,8,256]{3,2,1,0:T(8,128)}, f32[1,32,8,256]{3,2,1,0:T(8,128)}, f32[1,32,8,256]{3,2,1,0:T(8,128)}) custom-call(f32[2,32,8,256]{3,2,1,0:T(8,128)S(1)} %get-tuple-element.7.values, f32[16,1,128]{2,1,0:T(1,128)S(1)} %get-tuple-element.8.peak_in, s16[16,16,256]{2,1,0:T(8,128)(2,1)S(1)} %get-tuple-element.9.corr_in, ...), custom_call_target="tpu_custom_call" | custom-call | tf_op jit(solution)/shard_map/pallas_call | solution.py:644

commit v11 on v10

--- a/solution.py
+++ b/solution.py
@@ -57,12 +57,13 @@
     return square, np.concatenate(parts(halo), axis=0)
 
 
-def each_partner(body, near=0, row=None):
+def each_partner(body, near=0, row=None, up=0):
     me = lax.axis_index("shot")
     turn_x = (me < NS // 2).astype(jnp.int32)
     turn_y = (lax.rem(me, 4) < 2).astype(jnp.int32)
     turn_x = turn_x + near * (1 - 2 * turn_x)
     turn_y = turn_y + near * (1 - 2 * turn_y)
+    turn_x, turn_y = turn_x * (1 - up), turn_y * (1 - up)
     corner, step_x, step_y = 12 * turn_x + 3 * turn_y, 4 - 8 * turn_x, 1 - 2 * turn_y
 
     @pl.loop(0, 4)
@@ -323,7 +324,9 @@
     def _():
         halo_copy(3).start()
 
-    @pl.when(ty > 0)
+    later = (tx < 2) & (ty >= 4)
+
+    @pl.when((ty > 0) & jnp.logical_not(later))
     def _():
         halo_copy(1).start()
 
@@ -395,6 +398,10 @@
     def _(shot):
         blocks[shot] = serve(shot)
         block_copy(me, shot).start()
+
+    @pl.when(later)
+    def _():
+        halo_copy(1).start()
 
     arrived[me] = serve(me)
     @pl.when(ty >= 5)
@@ -513,7 +520,8 @@
                 four = arrived.at[pl.ds(4 * x, count)]
                 pltpu.make_async_copy(four, four, v_recv.at[x]).wait()
 
-    each_partner(one_owner, ((tx == 0) | (tx == 3)).astype(jnp.int32), row_of_blocks)
+    near = ((tx == 0) | (tx == 3)).astype(jnp.int32)
+    each_partner(one_owner, near, row_of_blocks, ((tx == 1) & direct).astype(jnp.int32))
 
     @pl.loop(0, CX)
     def _(r):

time: 27.6 us -> 29.3 us (1.062)
  the two profiles are of different devices: /device:TPU:1 before, /device:TPU:384 now
where the time goes in v11:
time: 29.3 us; the launch traced here: 29.2 us
  Pallas kernels  27.9 us (95%)
  between operations  1.29 us (4%)
    pallas_call x1, Pallas kernels, on_device(): pl.pallas_call(kernel, out_shape=(jax.ShapeDtypeStruct((2, CX, CY, CZ), f...  26.9 us
    pallas_call x1, Pallas kernels, on_device(): pl.pallas_call(finish, out_shape=(field, field, field), in_specs=[vmem] *...  0.99 us

profile of v11, /device:TPU:384, one launch (start us, length us, event | category | flops | bytes accessed | tf_op | source)
XLA Modules:
  0.0 29.2 jit_solution(9379022884682809607)
XLA Ops:
  1.3 26.9 %shard_map.139 = (f32[2,32,8,256]{3,2,1,0:T(8,128)S(1)}, f32[16,1,128]{2,1,0:T(1,128)S(1)}, s16[16,16,256]{2,1,0:T(8,128)(2,1)S(1)}, bf16[256,256]{1,0:T(8,128)(2,1)S(1)}) custom-call(f32[1,32,8,256]{3,2,1,0:T(8,128)} %f_prev.1, f32[1,32,8,256]{3,2,1,0:T(8,128)} %f_now.1, f32[1,32,8,256]{3,2,1,0:T(8,128)} %a_prev.1, f32[1,32,8,256]{3,2,1,0:T(8,128)} %a_now.1, ...), custom_call_target="tpu_custom_call" | custom-call | tf_op jit(solution)/shard_map/pallas_call | solution.py:637
  28.2 1.0 %shard_map.140 = (f32[1,32,8,256]{3,2,1,0:T(8,128)}, f32[1,32,8,256]{3,2,1,0:T(8,128)}, f32[1,32,8,256]{3,2,1,0:T(8,128)}) custom-call(f32[2,32,8,256]{3,2,1,0:T(8,128)S(1)} %get-tuple-element.7.values, f32[16,1,128]{2,1,0:T(1,128)S(1)} %get-tuple-element.8.peak_in, s16[16,16,256]{2,1,0:T(8,128)(2,1)S(1)} %get-tuple-element.9.corr_in, ...), custom_call_target="tpu_custom_call" | custom-call | tf_op jit(solution)/shard_map/pallas_call | solution.py:652

commit v12 on v11

--- a/solution.py
+++ b/solution.py
@@ -87,7 +87,7 @@
 def kernel(
     f_prev, f_now, a_prev, a_now, velocity, aperture, source_cell, strength, receivers, traces,
     square_hbm, halo_hbm,
-    prev, peak_in, corr_in, hit_out,
+    prev, peak_in, corr_in, hit_out, part,
     now, lap, high, low, edge_f, edge, far, slab_b, slab, ids, cell_v, trace_v, square, halo_w,
     pick_send, halo, tables, wanted, wanted_by, blocks, arrived, speed, peak_send, corr_send,
     hit,
@@ -324,9 +324,7 @@
     def _():
         halo_copy(3).start()
 
-    later = (tx < 2) & (ty >= 4)
-
-    @pl.when((ty > 0) & jnp.logical_not(later))
+    @pl.when(ty > 0)
     def _():
         halo_copy(1).start()
 
@@ -399,10 +397,6 @@
         blocks[shot] = serve(shot)
         block_copy(me, shot).start()
 
-    @pl.when(later)
-    def _():
-        halo_copy(1).start()
-
     arrived[me] = serve(me)
     @pl.when(ty >= 5)
     def _():
@@ -480,7 +474,7 @@
                 src_ref=source.at[owner],
                 dst_ref=target.at[me],
                 send_sem=c_send.at[n],
-                recv_sem=c_recv.at[n],
+                recv_sem=c_recv.at[2 * (me // 8) + n],
                 device_id={"shot": owner},
                 device_id_type=MESH,
             )
@@ -550,11 +544,29 @@
 
     all_sent(peak_send, c_send.at[0])
     all_sent(corr_send, c_send.at[1])
-    all_sent(peak_in, c_recv.at[0])
-    all_sent(corr_in, c_recv.at[1])
-
-
-def finish(values, peak_in, corr_in, hit, f_out, a_out, image_out, image, out_sem):
+    def arrive(half, count):
+        for n, ref in enumerate((peak_in, corr_in)):
+            some = ref.at[pl.ds(0, count)]
+            pltpu.make_async_copy(some, some, c_recv.at[2 * half + n]).wait()
+
+    arrive(me // 8, 7)
+    part[...] = image_of(me // 8, peak_in, corr_in, hit_out)
+    arrive(1 - me // 8, 8)
+
+
+def image_of(half, peak_in, corr_in, hit):
+    shots = pl.ds(8 * half, 8)
+    peak = peak_in[shots]
+    peak = jnp.broadcast_to(jnp.concatenate([peak, peak], axis=2), (8, 2 * CY, CZ))
+    share = corr_in[shots].astype(jnp.int32).astype(jnp.float32) * (1.0 / STEPS)
+    rows = (share * peak).reshape(ROWS // 2, CZ)
+    top = rows.astype(jnp.bfloat16)
+    rest = (rows - top.astype(jnp.float32)).astype(jnp.bfloat16)
+    chosen = hit[:, pl.ds(pl.multiple_of(ROWS // 2 * half, ROWS // 2), ROWS // 2)]
+    return mm(chosen, top) + mm(chosen, rest)
+
+
+def finish(values, peak_in, corr_in, hit, part, f_out, a_out, image_out, image, out_sem):
     outs = [
         pltpu.make_async_copy(values.at[0], f_out.at[0], out_sem.at[0]),
         pltpu.make_async_copy(values.at[1], a_out.at[0], out_sem.at[1]),
@@ -562,13 +574,9 @@
     ]
     outs[0].start()
     outs[1].start()
-    peak = peak_in[...]
-    peak = jnp.broadcast_to(jnp.concatenate([peak, peak], axis=2), (NS, 2 * CY, CZ))
-    share = corr_in[...].astype(jnp.int32).astype(jnp.float32) * (1.0 / STEPS)
-    rows = (share * peak).reshape(ROWS, CZ)
-    top = rows.astype(jnp.bfloat16)
-    rest = (rows - top.astype(jnp.float32)).astype(jnp.bfloat16)
-    image[...] = (mm(hit[...], top) + mm(hit[...], rest)).reshape(SLAB, CY, CZ)
+    half = 1 - lax.axis_index("shot") // 8
+    total = part[...] + image_of(half, peak_in, corr_in, hit)
+    image[...] = total.reshape(SLAB, CY, CZ)
     outs[2].start()
     for out in outs:
         out.wait()
@@ -628,22 +636,23 @@
         dma,
         dma((4,)),
         dma((2,)),
-        dma((2,)),
+        dma((4,)),
         pltpu.SemaphoreType.REGULAR((4,)),
         pltpu.SemaphoreType.REGULAR,
     ]
     anywhere = pl.BlockSpec(memory_space=pl.ANY)
     vmem = pl.BlockSpec(memory_space=pltpu.VMEM)
-    values, peak_in, corr_in, hit = pl.pallas_call(
+    results = pl.pallas_call(
         kernel,
         out_shape=(
             jax.ShapeDtypeStruct((2, CX, CY, CZ), f32),
             jax.ShapeDtypeStruct((NS, 1, CZ // 2), f32),
             jax.ShapeDtypeStruct((NS, 2 * CY, CZ), jnp.int16),
             jax.ShapeDtypeStruct((ROWS, ROWS), bf),
+            jax.ShapeDtypeStruct((ROWS, CZ), f32),
         ),
         in_specs=[anywhere] * 12,
-        out_specs=(vmem,) * 4,
+        out_specs=(vmem,) * 5,
         scratch_shapes=scratch,
         compiler_params=pltpu.CompilerParams(
             collective_id=0, has_side_effects=True, vmem_limit_bytes=LIMIT
@@ -652,11 +661,11 @@
     return pl.pallas_call(
         finish,
         out_shape=(field, field, field),
-        in_specs=[vmem] * 4,
+        in_specs=[vmem] * 5,
         out_specs=(anywhere,) * 3,
         scratch_shapes=[pltpu.VMEM((SLAB, CY, CZ), f32), dma((3,))],
         compiler_params=pltpu.CompilerParams(vmem_limit_bytes=LIMIT),
-    )(values, peak_in, corr_in, hit)
+    )(*results)
 
 
 def solution(mesh):

time: 29.3 us -> 27.6 us (0.942)
  the two profiles are of different devices: /device:TPU:384 before, /device:TPU:1 now
where the time goes in v12:
time: 27.6 us; the launch traced here: 27.5 us
  Pallas kernels  26.2 us (95%)
  between operations  1.29 us (5%)
    pallas_call x1, Pallas kernels, on_device(): pl.pallas_call(kernel, out_shape=(jax.ShapeDtypeStruct((2, CX, CY, CZ), f...  25.2 us
    pallas_call x1, Pallas kernels, on_device(): pl.pallas_call(finish, out_shape=(field, field, field), in_specs=[vmem] *...  0.98 us

profile of v12, /device:TPU:1, one launch (start us, length us, event | category | flops | bytes accessed | tf_op | source)
XLA Modules:
  0.0 27.5 jit_solution(5059635844010253971)
XLA Ops:
  1.3 25.2 %shard_map.139 = (f32[2,32,8,256]{3,2,1,0:T(8,128)S(1)}, f32[16,1,128]{2,1,0:T(1,128)S(1)}, s16[16,16,256]{2,1,0:T(8,128)(2,1)S(1)}, bf16[256,256]{1,0:T(8,128)(2,1)S(1)}, f32[256,256]{1,0:T(8,128)S(1)}) custom-call(f32[1,32,8,256]{3,2,1,0:T(8,128)} %f_prev.1, f32[1,32,8,256]{3,2,1,0:T(8,128)} %f_now.1, f32[1,32,8,256]{3,2,1,0:T(8,128)} %a_prev.1, ...), custom_call_target="tpu_custom_call" | custom-call | tf_op jit(solution)/shard_map/pallas_call | solution.py:645
  26.5 1.0 %shard_map.140 = (f32[1,32,8,256]{3,2,1,0:T(8,128)}, f32[1,32,8,256]{3,2,1,0:T(8,128)}, f32[1,32,8,256]{3,2,1,0:T(8,128)}) custom-call(f32[2,32,8,256]{3,2,1,0:T(8,128)S(1)} %get-tuple-element.8.values, f32[16,1,128]{2,1,0:T(1,128)S(1)} %get-tuple-element.9.peak_in, s16[16,16,256]{2,1,0:T(8,128)(2,1)S(1)} %get-tuple-element.10.corr_in, ...), custom_call_target="tpu_custom_call" | custom-call | tf_op jit(solution)/shard_map/pallas_call | solution.py:661

commit v13 on v12

--- a/solution.py
+++ b/solution.py
@@ -71,8 +71,7 @@
         if row is not None:
             row(3 * turn_x + (1 - 2 * turn_x) * i)
 
-        @pl.loop(0, 4)
-        def _(j):
+        for j in range(4):
             other = corner + step_x * i + step_y * j
 
             @pl.when(other != me)
@@ -92,7 +91,7 @@
     pick_send, halo, tables, wanted, wanted_by, blocks, arrived, speed, peak_send, corr_send,
     hit,
     smem_tables, source_s, strength_s,
-    load_sem, edge_sem, far_sem, table_sem, id_sem, id_send, id_recv, halo_send, halo_recv, v_send, v_recv,
+    load_sem, edge_sem, far_sem, table_sem, id_send, id_recv, halo_send, halo_recv, v_send, v_recv,
     c_send, c_recv, ready, go,
 ):
     me = lax.axis_index("shot")
@@ -388,7 +387,8 @@
 
     all_but_one = pl.ds(0, NS - 1)
     pltpu.make_async_copy(wanted.at[all_but_one], wanted.at[all_but_one], id_recv).wait()
-    id_local = pltpu.make_async_copy(wanted, wanted_by, id_sem)
+    table_copy.wait()
+    id_local = pltpu.make_async_copy(wanted, wanted_by, table_sem)
     id_local.start()
     id_local.wait()
 
@@ -466,7 +466,6 @@
                     weight = STENCIL_WEIGHTS[4 + q - x]
                     lap[field, CX - 4 + x] = lap[field, CX - 4 + x] + weight * far[field, q]
 
-    table_copy.wait()
 
     def corr_copies(owner):
         return [
@@ -630,7 +629,6 @@
         dma,
         dma,
         dma,
-        dma,
         dma((4,)),
         dma((4,)),
         dma,

time: 27.6 us -> 27.6 us (level)
  no operation moved by 1% of the time
where the time goes in v13:
time: 27.6 us; the launch traced here: 27.5 us
  Pallas kernels  26.2 us (95%)
  between operations  1.29 us (5%)
    pallas_call x1, Pallas kernels, on_device(): pl.pallas_call(kernel, out_shape=(jax.ShapeDtypeStruct((2, CX, CY, CZ), f...  25.2 us
    pallas_call x1, Pallas kernels, on_device(): pl.pallas_call(finish, out_shape=(field, field, field), in_specs=[vmem] *...  0.98 us

profile of v13, /device:TPU:1, one launch (start us, length us, event | category | flops | bytes accessed | tf_op | source)
XLA Modules:
  0.0 27.5 jit_solution(3988688905088571959)
XLA Ops:
  1.3 25.2 %shard_map.139 = (f32[2,32,8,256]{3,2,1,0:T(8,128)S(1)}, f32[16,1,128]{2,1,0:T(1,128)S(1)}, s16[16,16,256]{2,1,0:T(8,128)(2,1)S(1)}, bf16[256,256]{1,0:T(8,128)(2,1)S(1)}, f32[256,256]{1,0:T(8,128)S(1)}) custom-call(f32[1,32,8,256]{3,2,1,0:T(8,128)} %f_prev.1, f32[1,32,8,256]{3,2,1,0:T(8,128)} %f_now.1, f32[1,32,8,256]{3,2,1,0:T(8,128)} %a_prev.1, ...), custom_call_target="tpu_custom_call" | custom-call | tf_op jit(solution)/shard_map/pallas_call | solution.py:643
  26.5 1.0 %shard_map.140 = (f32[1,32,8,256]{3,2,1,0:T(8,128)}, f32[1,32,8,256]{3,2,1,0:T(8,128)}, f32[1,32,8,256]{3,2,1,0:T(8,128)}) custom-call(f32[2,32,8,256]{3,2,1,0:T(8,128)S(1)} %get-tuple-element.8.values, f32[16,1,128]{2,1,0:T(1,128)S(1)} %get-tuple-element.9.peak_in, s16[16,16,256]{2,1,0:T(8,128)(2,1)S(1)} %get-tuple-element.10.corr_in, ...), custom_call_target="tpu_custom_call" | custom-call | tf_op jit(solution)/shard_map/pallas_call | solution.py:659

commit v14 on v13

--- a/solution.py
+++ b/solution.py
@@ -566,19 +566,19 @@
 
 
 def finish(values, peak_in, corr_in, hit, part, f_out, a_out, image_out, image, out_sem):
-    outs = [
-        pltpu.make_async_copy(values.at[0], f_out.at[0], out_sem.at[0]),
-        pltpu.make_async_copy(values.at[1], a_out.at[0], out_sem.at[1]),
-        pltpu.make_async_copy(image, image_out.at[0], out_sem.at[2]),
-    ]
-    outs[0].start()
-    outs[1].start()
+    def write(n, source, target):
+        for part_of in range(4):
+            rows = pl.ds(8 * part_of, 8)
+            pltpu.make_async_copy(source.at[rows], target.at[0, rows], out_sem.at[n]).start()
+
+    write(0, values.at[0], f_out)
+    write(1, values.at[1], a_out)
     half = 1 - lax.axis_index("shot") // 8
     total = part[...] + image_of(half, peak_in, corr_in, hit)
     image[...] = total.reshape(SLAB, CY, CZ)
-    outs[2].start()
-    for out in outs:
-        out.wait()
+    write(2, image, image_out)
+    for n, target in enumerate((f_out, a_out, image_out)):
+        pltpu.make_async_copy(image, target.at[0], out_sem.at[n]).wait()
 
 
 def on_device(*arrays):

time: 27.6 us -> 27.6 us (level)
  no operation moved by 1% of the time
where the time goes in v14:
time: 27.6 us; the launch traced here: 27.4 us
  Pallas kernels  26.2 us (95%)
  between operations  1.29 us (5%)
    pallas_call x1, Pallas kernels, on_device(): pl.pallas_call(kernel, out_shape=(jax.ShapeDtypeStruct((2, CX, CY, CZ), f...  25.2 us
    pallas_call x1, Pallas kernels, on_device(): pl.pallas_call(finish, out_shape=(field, field, field), in_specs=[vmem] *...  0.97 us

profile of v14, /device:TPU:1, one launch (start us, length us, event | category | flops | bytes accessed | tf_op | source)
XLA Modules:
  0.0 27.4 jit_solution(14817590397133134733)
XLA Ops:
  1.3 25.2 %shard_map.139 = (f32[2,32,8,256]{3,2,1,0:T(8,128)S(1)}, f32[16,1,128]{2,1,0:T(1,128)S(1)}, s16[16,16,256]{2,1,0:T(8,128)(2,1)S(1)}, bf16[256,256]{1,0:T(8,128)(2,1)S(1)}, f32[256,256]{1,0:T(8,128)S(1)}) custom-call(f32[1,32,8,256]{3,2,1,0:T(8,128)} %f_prev.1, f32[1,32,8,256]{3,2,1,0:T(8,128)} %f_now.1, f32[1,32,8,256]{3,2,1,0:T(8,128)} %a_prev.1, ...), custom_call_target="tpu_custom_call" | custom-call | tf_op jit(solution)/shard_map/pallas_call | solution.py:643
  26.5 1.0 %shard_map.140 = (f32[1,32,8,256]{3,2,1,0:T(8,128)}, f32[1,32,8,256]{3,2,1,0:T(8,128)}, f32[1,32,8,256]{3,2,1,0:T(8,128)}) custom-call(f32[2,32,8,256]{3,2,1,0:T(8,128)S(1)} %get-tuple-element.8.values, f32[16,1,128]{2,1,0:T(1,128)S(1)} %get-tuple-element.9.peak_in, s16[16,16,256]{2,1,0:T(8,128)(2,1)S(1)} %get-tuple-element.10.corr_in, ...), custom_call_target="tpu_custom_call" | custom-call | tf_op jit(solution)/shard_map/pallas_call | solution.py:659

commit v15 on v14

--- a/solution.py
+++ b/solution.py
@@ -233,10 +233,6 @@
         pltpu.make_async_copy(edge_f, edge_f, edge_sem).wait()
         edge[...] = edge_f[...].reshape(2, XH, CZ).astype(jnp.bfloat16)
 
-    @pl.when(relayed & (ty >= DIRECT) & jnp.logical_not(mutual))
-    def _():
-        across()
-
     pltpu.make_async_copy(now, now, load_sem.at[1]).wait()
 
     @pl.loop(0, 2)
@@ -282,6 +278,10 @@
         pl.semaphore_signal(go, inc=1, device_id={"tx": 2}, device_id_type=MESH)
 
     upper = me // 4 + lax.rem(me, 4) >= 2
+
+    @pl.when(relayed & (ty >= DIRECT) & jnp.logical_not(mutual))
+    def _():
+        across()
 
     @pl.when(relayed & mutual & jnp.logical_not(upper))
     def _():

time: 27.6 us -> 27.4 us (level)
  no operation moved by 1% of the time
where the time goes in v15:
time: 27.4 us; the launch traced here: 27.3 us
  Pallas kernels  26 us (95%)
  between operations  1.29 us (5%)
    pallas_call x1, Pallas kernels, on_device(): pl.pallas_call(kernel, out_shape=(jax.ShapeDtypeStruct((2, CX, CY, CZ), f...  25 us
    pallas_call x1, Pallas kernels, on_device(): pl.pallas_call(finish, out_shape=(field, field, field), in_specs=[vmem] *...  0.97 us

profile of v15, /device:TPU:1, one launch (start us, length us, event | category | flops | bytes accessed | tf_op | source)
XLA Modules:
  0.0 27.3 jit_solution(12004409182464484415)
XLA Ops:
  1.3 25.0 %shard_map.139 = (f32[2,32,8,256]{3,2,1,0:T(8,128)S(1)}, f32[16,1,128]{2,1,0:T(1,128)S(1)}, s16[16,16,256]{2,1,0:T(8,128)(2,1)S(1)}, bf16[256,256]{1,0:T(8,128)(2,1)S(1)}, f32[256,256]{1,0:T(8,128)S(1)}) custom-call(f32[1,32,8,256]{3,2,1,0:T(8,128)} %f_prev.1, f32[1,32,8,256]{3,2,1,0:T(8,128)} %f_now.1, f32[1,32,8,256]{3,2,1,0:T(8,128)} %a_prev.1, ...), custom_call_target="tpu_custom_call" | custom-call | tf_op jit(solution)/shard_map/pallas_call | solution.py:643
  26.3 1.0 %shard_map.140 = (f32[1,32,8,256]{3,2,1,0:T(8,128)}, f32[1,32,8,256]{3,2,1,0:T(8,128)}, f32[1,32,8,256]{3,2,1,0:T(8,128)}) custom-call(f32[2,32,8,256]{3,2,1,0:T(8,128)S(1)} %get-tuple-element.8.values, f32[16,1,128]{2,1,0:T(1,128)S(1)} %get-tuple-element.9.peak_in, s16[16,16,256]{2,1,0:T(8,128)(2,1)S(1)} %get-tuple-element.10.corr_in, ...), custom_call_target="tpu_custom_call" | custom-call | tf_op jit(solution)/shard_map/pallas_call | solution.py:659
